TPU v7x, 32 devices: a whole 2x2x4 slice. The times are simulated.
32 devices in a mesh: leaf: 16 (over z, y, x), sub: 2 (over core).
Axes of the slice: x: 2, y: 2, z: 4, core: 2. Of those that a mesh axis runs over, the one named last changes fastest.
Arguments:
- right_sides: float32 [2, 4, 16, 1536], P(None, None, None, ('leaf', 'sub')), may hold values from -6 to 6
- diag_inverse: float32 [2, 1536, 2880], P(None, ('leaf', 'sub'))
- coupling: float32 [2, 1536, 1344], P(None, ('leaf', 'sub'))
- boundary: int32 [32, 1344], P(('leaf', 'sub')), may hold values from 0 to 2687, as said below
- plane_map: int32 [32, 192], P(('leaf', 'sub')), may hold values from 0 to 191, each once within a row
Outputs:
- plane_field: float32 [2, 16, 6144], P(None, None, ('leaf', 'sub'))
Inputs may be any that keep to these rules, and one draw needn't show every extreme that they name: `boundary`: for level l >= 1 (columns e_l .. e_l + n_l - 1 of a row), entries lie in 0 .. (sum of n_a over a < l) - 1 and are equal on all devices d with the same d div (32 / 2^l); the first entry of each such segment is its largest allowed value and the second is 0.
All inputs are finite; a program needn't handle non-finite values.
Results may differ from a plain program's by a relative error of at most 0.0001.
Values sent between devices are 32-bit elements; how exact they have to be, the bound alone decides.
No kernel may reach another device: no remote copies, remote signals or barrier semaphores. Data moves between devices by JAX's collectives and lax.ppermute only.
A program may use at most 64 MiB of HBM per device.

v0:
```python
import functools

import jax
import jax.numpy as jnp
from jax import lax
from jax.experimental import pallas as pl
from jax.experimental.pallas import tpu as pltpu
from jax.sharding import PartitionSpec as P


LEVELS = 4
LANES = 128
AXES = ("leaf", "sub")


def round_up(value, step):
    return -(-value // step) * step


def roll_left(block, shift):
    shift = shift % LANES
    return block if shift == 0 else pltpu.roll(block, LANES - shift, axis=block.ndim - 1)


def roll_right(block, shift):
    return roll_left(block, LANES - shift % LANES)


def lane_of(shape):
    return lax.broadcasted_iota(jnp.int32, shape, len(shape) - 1)


def split(matrix):
    high = matrix.astype(jnp.bfloat16)
    rest = matrix - high.astype(jnp.float32)
    mid = rest.astype(jnp.bfloat16)
    low = (rest - mid.astype(jnp.float32)).astype(jnp.bfloat16)
    return [high, mid, low]


def weights(vectors, width):
    vectors = jnp.where(lane_of(vectors.shape) < width, vectors, 0.0)
    high = vectors.astype(jnp.bfloat16).astype(jnp.float32)
    rest = vectors - high
    mid = rest.astype(jnp.bfloat16).astype(jnp.float32)
    low = rest - mid
    return (high + roll_right(mid, width) + roll_right(low, 2 * width)).astype(jnp.bfloat16)


def product(real, imag, packed, width):
    rows = real.shape[0]
    stacked = jnp.concatenate(split(real) + split(imag), axis=0)
    terms = jnp.dot(stacked, packed, preferred_element_type=jnp.float32)

    def total(first):
        part = terms[first * rows : (first + 1) * rows]
        part = part + terms[(first + 1) * rows : (first + 2) * rows]
        part = part + terms[(first + 2) * rows : (first + 3) * rows]
        return part + roll_left(part, width) + roll_left(part, 2 * width)

    by_real, by_imag = total(0), total(3)
    half = width // 2
    swapped = jnp.where(
        lane_of(by_imag.shape) < half, -roll_left(by_imag, half), roll_right(by_imag, half)
    )
    return by_real + swapped


def side_by_side(blocks, width):
    lane = lane_of(blocks[0].shape)
    packed = jnp.where(lane < width, blocks[0], 0.0)
    for at in range(1, len(blocks)):
        inside = (lane >= at * width) & (lane < (at + 1) * width)
        packed = jnp.where(inside, roll_right(blocks[at], at * width), packed)
    return packed


def gather_rows(source, index, first, count, target):
    step = 8

    def body(turn, carry):
        for inner in range(step):
            row = turn * step + inner
            target[pl.ds(row, 1), :] = source[pl.ds(index[0, first + row], 1), :]
        return carry

    lax.fori_loop(0, count // step, body, 0)


def spread(wires, target, base, local, flips, lanes_flips, rows, width):
    for entry, flip in enumerate(flips):
        for lane_block, lane_flip in enumerate(lanes_flips):
            place = pl.multiple_of(base + (local ^ (flip ^ lane_flip)) * rows, 8)
            target[pl.ds(place, rows), :] = roll_left(wires[entry], lane_block * width)


class Plan:
    def __init__(self, total, leafs, rows, sources):
        self.total, self.leafs, self.rows, self.sources = total, leafs, rows, sources
        self.width = 2 * sources
        self.members = [total >> level for level in range(LEVELS)]
        self.order = [members * rows for members in self.members]
        self.group_rows = round_up(-(-rows // (LANES // self.width)), 8)
        self.groups = -(-rows // self.group_rows)
        self.couple_at = [0, 0]
        for level in range(1, LEVELS):
            self.couple_at.append(self.couple_at[-1] + self.order[level])
        self.couple = self.couple_at[LEVELS]
        self.ancestors = [sum(self.order[:level]) for level in range(LEVELS + 1)]
        own = (LEVELS - 1) * sources
        at = self.couple
        self.rhs_at = at if at % LANES + own <= LANES else round_up(at, LANES)
        self.couple_wide = round_up(self.rhs_at + own, LANES)
        self.flips = [0, 2, 4, 6]

    def shared(self, level):
        return [flip for flip in self.flips if flip < self.members[level]]

    def open_bits(self, level):
        bits = range(self.members[level].bit_length() - 1)
        return [bit for bit in bits if (1 << bit) not in (2, 4)]

    def local(self, level):
        position = lax.axis_index("leaf") * (self.total // self.leafs) + lax.axis_index("sub")
        return position & (self.members[level] - 1)


def transposed(block, scratch):
    scratch[...] = jnp.zeros_like(scratch)
    scratch[0 : block.shape[0], 0 : block.shape[1]] = block
    return scratch[...].T


def rhs_kernel(plan, rhs, wire, late, scratch):
    rows = plan.rows
    first = jnp.concatenate([rhs[0, 0], rhs[1, 0]], axis=0)
    first = transposed(first, scratch)
    padded = plan.groups * plan.group_rows
    blocks = [first[at : at + plan.group_rows] for at in range(0, padded, plan.group_rows)]
    packed = side_by_side(blocks, plan.width)
    wire[...] = jnp.broadcast_to(packed[None], wire.shape)
    for part in range(2):
        later = jnp.concatenate([rhs[part, level] for level in range(1, LEVELS)], axis=0)
        late[part] = transposed(later, scratch)[0:rows]


def coupling_kernel(plan, coupling, late, joined):
    whole = plan.couple // LANES * LANES
    tail = plan.couple - whole
    shift = plan.rhs_at % LANES
    for part in range(2):
        joined[part, :, 0:whole] = coupling[part, :, 0:whole]
        joined[part, :, plan.couple_wide - LANES :] = roll_right(late[part], shift)
        if tail:
            joined[part, :, whole : whole + tail] = coupling[part, :, whole : whole + tail]


def rhs_rows(plan, real, imag, level, shift_cols):
    start = plan.rhs_at // LANES * LANES - shift_cols
    offset = plan.rhs_at % LANES + plan.sources * (level - 1)
    re_part = roll_left(real[:, start : start + LANES], offset)
    im_part = roll_left(imag[:, start : start + LANES], offset - plan.sources)
    return jnp.where(lane_of(re_part.shape) < plan.sources, re_part, im_part)


def unpack_all(plan, near, far, target):
    g = plan.group_rows
    core = lax.axis_index("sub")
    for place, wires in ((core, near), (core ^ 1, far)):
        flat = wires[...].reshape(plan.leafs * g, LANES)
        for group in range(plan.groups):
            block = roll_left(flat, group * plan.width).reshape(plan.leafs, g, LANES)
            count = min(g, plan.rows - group * g)
            target[:, place, group * g : group * g + count, :] = block[:, 0:count]


def pack_all(plan, rows_block, wire):
    g = plan.group_rows
    padded = plan.groups * g
    if padded > plan.rows:
        extra = jnp.zeros((padded - plan.rows, LANES), jnp.float32)
        rows_block = jnp.concatenate([rows_block, extra], axis=0)
    blocks = [rows_block[at : at + g] for at in range(0, padded, g)]
    wire[...] = jnp.broadcast_to(side_by_side(blocks, plan.width)[None], wire.shape)


def top_kernel(plan, near, far, diag, wire, vector):
    unpack_all(plan, near, far, vector)
    packed = weights(vector[...].reshape(plan.order[0], LANES), plan.width)
    pack_all(plan, product(diag[0], diag[1], packed, plan.width), wire)


def reduce_rows(plan, level, blocks, packed_first_col, packed):
    out = []
    first = plan.couple_at[level] - packed_first_col
    for real, imag in blocks:
        cols = slice(first, first + plan.order[level])
        value = product(real[:, cols], imag[:, cols], packed, plan.width)
        out.append(rhs_rows(plan, real, imag, level, packed_first_col) - value)
    return out


def first_reduce_kernel(
    plan, near, far, index, own, from_x, from_y, diag_re, diag_im, wire, top, rest, bounds
):
    unpack_all(plan, near, far, top)
    gather_rows(
        top.reshape(plan.order[0], LANES), index, plan.couple_at[1], plan.order[1], bounds
    )
    blocks = [
        (own.at[0], own.at[1]),
        (from_x.at[0], from_x.at[1]),
        (from_y.at[0], from_y.at[1]),
        (diag_re, diag_im),
    ]
    packed = weights(bounds[...], plan.width)
    wire[...] = side_by_side(reduce_rows(plan, 1, blocks, 0, packed), plan.width)
    for at, (real, imag) in enumerate(blocks):
        rest[at, 0] = real[:, plan.order[1] :]
        rest[at, 1] = imag[:, plan.order[1] :]


def first_solve_kernel(plan, flips, wires, own, from_x, from_y, diag_re, diag_im, wire, rest, vector):
    order = plan.order[1]
    spread(wires, vector, 0, plan.local(1), flips, plan.shared(1), plan.rows, plan.width)
    packed = weights(vector[...], plan.width)
    blocks = [
        (own.at[0], own.at[1]),
        (from_x.at[0], from_x.at[1]),
        (from_y.at[0], from_y.at[1]),
        (diag_re, diag_im),
    ]
    solved = [product(re[:, 0:order], im[:, 0:order], packed, plan.width) for re, im in blocks]
    wire[...] = side_by_side(solved, plan.width)
    for at, (real, imag) in enumerate(blocks):
        rest[at, 0] = real[:, order:]
        rest[at, 1] = imag[:, order:]


def pack_owners(plan, row_map, local_rows, packing, out):
    slots = plan.rows * LEVELS // plan.leafs
    per_row = LANES // plan.width
    packing[...] = jnp.zeros_like(packing)

    def body(owner, carry):
        for slot in range(slots):
            row = row_map[0, owner * slots + slot]
            packing[slot % per_row, owner, pl.ds(slot // per_row, 1), :] = local_rows[
                pl.ds(row, 1), :
            ]
        return carry

    lax.fori_loop(0, plan.leafs, body, 0)
    lane = lane_of(out.shape)
    total = jnp.where(lane < plan.width, packing[0], 0.0)
    for at in range(1, per_row):
        inside = (lane >= at * plan.width) & (lane < (at + 1) * plan.width)
        total = jnp.where(inside, roll_right(packing[at], at * plan.width), total)
    out[...] = total


def own_rows(plan, vector, level):
    place = pl.multiple_of(plan.ancestors[level] + plan.local(level) * plan.rows, 8)
    return vector[pl.ds(place, plan.rows), :]


def tail_kernel(
    plan, flips, top, wires, index, row_map, couple, couple_far, diag, diag_far, diag_last,
    out, vector, bounds, front, local_rows, packing,
):
    rows, width = plan.rows, plan.width
    vector[0 : plan.order[0], :] = top[...]
    spread(wires, vector, plan.order[0], plan.local(1), flips, plan.shared(1), rows, width)
    cut = plan.order[1]

    def held(level):
        found = []
        for at, flip in enumerate(plan.shared(level)):
            found.append((flip, couple.at[at], diag.at[at]))
            found.append((flip ^ 1, couple_far.at[at], diag_far.at[at]))
        return found

    for level in range(2, LEVELS):
        order = plan.order[level]
        local = plan.local(level)
        gather_rows(vector, index, plan.couple_at[level], order, bounds)
        packed = weights(bounds[0:order, :], width)
        blocks = [(pair.at[0], pair.at[1]) for _, pair, _ in held(level)]
        reduced = reduce_rows(plan, level, blocks, cut, packed)
        for (flip, _, _), value in zip(held(level), reduced):
            front[pl.ds(pl.multiple_of((local ^ flip) * rows, 8), rows), :] = value
        packed = weights(front[0:order, :], width)
        base = plan.ancestors[level]
        if level + 1 < LEVELS:
            for flip, _, pair in held(level):
                solved = product(pair[0], pair[1], packed, width)
                place = pl.multiple_of(base + (local ^ flip) * rows, 8)
                vector[pl.ds(place, rows), :] = solved
        else:
            local_rows[level * rows :, :] = product(diag_last[0], diag_last[1], packed, width)
    for level in range(LEVELS - 1):
        local_rows[level * rows : (level + 1) * rows, :] = own_rows(plan, vector, level)
    pack_owners(plan, row_map, local_rows, packing, out)


def reduce_kernel(plan, level, flips, top, wires, index, couple, wire, vector, bounds):
    rows, width = plan.rows, plan.width
    vector[0 : plan.ancestors[level - 1], :] = top[...]
    spread(
        wires, vector, plan.ancestors[level - 1], plan.local(level - 1), flips,
        plan.shared(level - 1), rows, width,
    )
    gather_rows(vector, index, plan.couple_at[level], plan.order[level], bounds)
    blocks = [(couple.at[at, 0], couple.at[at, 1]) for at in range(len(plan.shared(level)))]
    packed = weights(bounds[...], width)
    wire[...] = side_by_side(reduce_rows(plan, level, blocks, plan.order[1], packed), width)


def solve_kernel(plan, level, flips, first_col, wires, diag, wire, vector):
    spread(wires, vector, 0, plan.local(level), flips, plan.shared(level), plan.rows, plan.width)
    packed = weights(vector[...], plan.width)
    cols = slice(first_col, first_col + plan.order[level])
    solved = [
        product(diag[at, 0, :, cols], diag[at, 1, :, cols], packed, plan.width)
        for at in range(len(plan.shared(level)))
    ]
    wire[...] = side_by_side(solved, plan.width)


def last_kernel(plan, flips, top, wires, row_map, diag_last, out, front, local_rows, packing):
    level = LEVELS - 1
    rows, width = plan.rows, plan.width
    spread(wires, front, 0, plan.local(level), flips, plan.shared(level), rows, width)
    packed = weights(front[...], width)
    local_rows[level * rows :, :] = product(diag_last[0], diag_last[1], packed, width)
    for upper in range(level):
        local_rows[upper * rows : (upper + 1) * rows, :] = own_rows(plan, top, upper)
    pack_owners(plan, row_map, local_rows, packing, out)


def owner_kernel(plan, received, out, scratch):
    slots = plan.rows * LEVELS // plan.leafs
    per_row = LANES // plan.width
    for slot in range(slots):
        block = roll_left(received[:, slot // per_row, :], slot % per_row * plan.width)
        scratch[pl.ds(slot, plan.leafs, stride=slots), :] = block
    out[...] = scratch[...].T[0 : plan.width]


def call(kernel, plan, outs, scratch, args, scalars=(), static=()):
    specs = []
    for at in range(len(args)):
        space = pltpu.SMEM if at in scalars else pltpu.VMEM
        specs.append(pl.BlockSpec(memory_space=space))
    shapes = [jax.ShapeDtypeStruct(shape, jnp.float32) for shape in outs]
    return pl.pallas_call(
        functools.partial(kernel, plan, *static),
        out_shape=shapes,
        in_specs=specs,
        out_specs=[pl.BlockSpec(memory_space=pltpu.VMEM)] * len(outs),
        scratch_shapes=[pltpu.VMEM(shape, jnp.float32) for shape in scratch],
        compiler_params=pltpu.CompilerParams(vmem_limit_bytes=16 << 20),
    )(*args)


def local(right_sides, diag_inverse, coupling, boundary, plane_map):
    total = lax.axis_size(AXES)
    leafs = lax.axis_size("leaf")
    sources, rows = right_sides.shape[2], right_sides.shape[3]
    plan = Plan(total, leafs, rows, sources)
    order = plan.order
    per_row = LANES // plan.width
    owner_rows = -(-(rows * LEVELS // leafs) // per_row)
    packing = (per_row, leafs, owner_rows, LANES)
    wire_shape = (leafs, plan.group_rows, LANES)
    whole_shape = (leafs, total // leafs, rows, LANES)
    block = (rows, LANES)

    def hop(array, bit):
        route = [(device, device ^ (1 << bit)) for device in range(total)]
        return lax.ppermute(array, AXES, route)

    def exchange(wire, level):
        current, flips = wire[None], [0]
        for bit in plan.open_bits(level):
            found = hop(current, bit)
            current = jnp.concatenate([current, found], axis=0)
            flips = flips + [flip ^ (1 << bit) for flip in flips]
        return current, flips

    def to_all(wire):
        near = lax.all_to_all(wire, "leaf", 0, 0)
        return near, hop(near, 0)

    def neighbours(array):
        return array, hop(array, 1), hop(array, 2)

    def beyond(pieces):
        own, from_x, from_y = pieces
        real = hop(from_x[0], 2)
        return (own, from_x, from_y, real, hop(from_y[1], 1))

    diag_top = diag_inverse[:, :, : order[0]]
    middle = sum(order[:-1])
    diag_mid = diag_inverse[:, :, order[0] : middle]
    diag_last = diag_inverse[:, :, middle:]

    wire, late = call(
        rhs_kernel, plan, [wire_shape, (2, rows, LANES)], [(LANES, LANES)], [right_sides]
    )
    (joined,) = call(coupling_kernel, plan, [(2, rows, plan.couple_wide)], [], [coupling, late])
    gathered = to_all(wire)
    couple = beyond(neighbours(joined))
    (wire,) = call(top_kernel, plan, [wire_shape], [whole_shape], [*gathered, diag_top])
    gathered = to_all(wire)
    diag = beyond(neighbours(diag_mid))
    wire, top, couple_rest = call(
        first_reduce_kernel, plan,
        [block, whole_shape, (4, 2, rows, plan.couple_wide - order[1])],
        [(order[1], LANES)],
        [*gathered, boundary, *couple], scalars=(2,),
    )
    top = top.reshape(order[0], LANES)
    wires, flips = exchange(wire, 1)
    wire, diag_rest = call(
        first_solve_kernel, plan, [block, (4, 2, rows, diag_mid.shape[2] - order[1])],
        [(order[1], LANES)], [wires, *diag], static=(flips,),
    )
    wires, flips = exchange(wire, 1)
    if plan.members[2] <= 8:
        couple_far = hop(couple_rest, 0)
        diag_far = hop(diag_rest, 0)
        (packed,) = call(
            tail_kernel, plan, [(leafs, owner_rows, LANES)],
            [
                (plan.ancestors[LEVELS - 1], LANES), (order[2], LANES), (order[2], LANES),
                (LEVELS * rows, LANES), packing,
            ],
            [
                top, wires, boundary, plane_map, couple_rest, couple_far, diag_rest, diag_far,
                diag_last,
            ],
            scalars=(2, 3), static=(flips,),
        )
    else:
        first_col = 0
        for level in range(2, LEVELS):
            wire, top = call(
                reduce_kernel, plan, [block, (plan.ancestors[level], LANES)],
                [(order[level], LANES)],
                [top, wires, boundary, couple_rest], scalars=(2,), static=(level, flips),
            )
            wires, flips = exchange(wire, level)
            if level + 1 < LEVELS:
                (wire,) = call(
                    solve_kernel, plan, [block], [(order[level], LANES)],
                    [wires, diag_rest], static=(level, flips, first_col),
                )
                first_col += order[level]
                wires, flips = exchange(wire, level)
        (packed,) = call(
            last_kernel, plan, [(leafs, owner_rows, LANES)],
            [(order[-1], LANES), (LEVELS * rows, LANES), packing],
            [top, wires, plane_map, diag_last], scalars=(2,), static=(flips,),
        )
    received = lax.all_to_all(packed, "leaf", 0, 0)
    (field,) = call(
        owner_kernel, plan, [(plan.width, LEVELS * rows)], [(LEVELS * rows, LANES)], [received]
    )
    return field.reshape(2, sources, LEVELS * rows)


def solution(mesh):
    in_specs = (
        P(None, None, None, AXES),
        P(None, AXES, None),
        P(None, AXES, None),
        P(AXES, None),
        P(AXES, None),
    )
    out_specs = P(None, None, AXES)
    return jax.shard_map(local, mesh=mesh, in_specs=in_specs, out_specs=out_specs, check_vma=False)
```

profile of v0, /device:TPU:0, one launch (start us, length us, event | category | flops | bytes accessed | tf_op | source)
XLA Modules:
  0.0 89.1 jit_solution(5428192583581876261)
XLA Ops:
  0.0 0.0 copy-start.1
  0.0 0.8 copy-done.1
  0.8 0.2 shard_map.55
  1.0 0.0 copy-start
  1.0 1.1 %copy-done = f32[2,48,1344]{2,1,0:T(8,128)S(1)} copy-done((f32[2,48,1344]{2,1,0:T(8,128)S(1)}, f32[2,48,1344]{2,1,0:T(8,128)}, u32[]{:S(2)}) %copy-start) | copy-done | bytes 516120
  2.1 0.0 copy-start.4
  2.1 0.1 shard_map.57.own
  2.2 3.0 %collective-permute-start.2 = (f32[2,48,1408]{2,1,0:T(8,128)S(1)}, f32[2,48,1408]{2,1,0:T(8,128)S(1)}, u32[]{:S(2)}, u32[]{:S(2)}) collective-permute-start(f32[2,48,1408]{2,1,0:T(8,128)S(1)} %shard_map.57.own), channel_id=1, source_target_pairs={{0,2},{1,3},{2,0},{3,1},{4,6},{5,7},{6,4},{7,5},{8,10},{9,11},{10,... | collective-permute-start | bytes 1622024 | tf_op jit(solution)/shard_map/ppermute | solution.py:381
  5.2 14.8 %all_to_all.15.near = f32[16,16,128]{2,1,0:T(8,128)S(1)} all-to-all(f32[16,16,128]{2,1,0:T(8,128)S(1)} %get-tuple-element.12), channel_id=1, replica_groups=mesh['leaf'=16,'sub'=2] {'leaf'}, dimensions={0} | all-to-all | bytes 262144 | tf_op jit(solution)/shard_map/all_to_all | solution.py:392
  20.0 0.0 collective-permute-start
  20.0 0.7 collective-permute-start.3
  20.6 0.0 copy-done.4
  20.7 1.5 %collective-permute-start.8 = (f32[2,48,1152]{2,1,0:T(8,128)S(1)}, f32[2,48,1152]{2,1,0:T(8,128)S(1)}, u32[]{:S(2)}, u32[]{:S(2)}) collective-permute-start(f32[2,48,1152]{2,1,0:T(8,128)S(1)} %slice.24.own), channel_id=1, source_target_pairs={{0,2},{1,3},{2,0},{3,1},{4,6},{5,7},{6,4},{7,5},{8,10},{9,11},{10,... | collective-permute-start | bytes 1327112 | tf_op jit(solution)/shard_map/ppermute | solution.py:381
  22.2 1.5 %collective-permute-start.9 = (f32[2,48,1152]{2,1,0:T(8,128)S(1)}, f32[2,48,1152]{2,1,0:T(8,128)S(1)}, u32[]{:S(2)}, u32[]{:S(2)}) collective-permute-start(f32[2,48,1152]{2,1,0:T(8,128)S(1)} %slice.24.own), channel_id=1, source_target_pairs={{0,4},{1,5},{2,6},{3,7},{4,0},{5,1},{6,2},{7,3},{8,12},{9,13},{10,... | collective-permute-start | bytes 1327112 | tf_op jit(solution)/shard_map/ppermute | solution.py:381
  23.8 0.0 collective-permute-done.far
  23.8 1.7 %shard_map.56 = f32[16,16,128]{2,1,0:T(8,128)} custom-call(f32[16,16,128]{2,1,0:T(8,128)S(1)} %all_to_all.15.near, f32[16,16,128]{2,1,0:T(8,128)S(1)} %collective-permute-done.far, f32[2,48,1536]{2,1,0:T(8,128)S(1)} %slice.21.diag), custom_call_target="tpu_custom_call" | custom-call | tf_op jit(solution)/shard_map/pallas_call | solution.py:356
  25.5 0.0 copy-start.2
  25.5 5.1 %all-to-all-start.1 = ((f32[16,16,128]{2,1,0:T(8,128)}), f32[16,16,128]{2,1,0:T(8,128)S(1)}, u32[]{:S(2)}, u32[]{:S(2)}) async-start(f32[16,16,128]{2,1,0:T(8,128)} %shard_map.56), calls=%async_computation.1 | async-start | bytes 262144 | tf_op jit(solution)/shard_map/all_to_all | solution.py:392
  30.6 0.0 collective-permute-done.2.from_x
  30.6 0.7 slice_bitcast_fusion.1
  31.3 1.9 %collective-permute-start.4 = (f32[48,1408]{1,0:T(8,128)}, f32[48,1408]{1,0:T(8,128)S(1)}, u32[]{:S(2)}, u32[]{:S(2)}) collective-permute-start(f32[48,1408]{1,0:T(8,128)} %slice_bitcast_fusion.1), channel_id=1, source_target_pairs={{0,4},{1,5},{2,6},{3,7},{4,0},{5,1},{6,2},{7,3},{8,12},{9,13},{10,... | collective-permute-start | bytes 811016 | tf_op jit(solution)/shard_map/ppermute | solution.py:381
  33.3 2.4 %collective-permute-done.3.from_y = f32[2,48,1408]{2,1,0:T(8,128)S(1)} collective-permute-done((f32[2,48,1408]{2,1,0:T(8,128)S(1)}, f32[2,48,1408]{2,1,0:T(8,128)S(1)}, u32[]{:S(2)}, u32[]{:S(2)}) %collective-permute-start.3) | collective-permute-done | bytes 540704 | tf_op jit(solution)/shard_map/ppermute | solution.py:381
  35.7 0.7 slice_bitcast_fusion
  36.4 1.8 %collective-permute-start.5 = (f32[48,1408]{1,0:T(8,128)}, f32[48,1408]{1,0:T(8,128)}, u32[]{:S(2)}, u32[]{:S(2)}) collective-permute-start(f32[48,1408]{1,0:T(8,128)} %slice_bitcast_fusion), channel_id=1, source_target_pairs={{0,2},{1,3},{2,0},{3,1},{4,6},{5,7},{6,4},{7,5},{8,10},{9,11},{10,... | collective-permute-start | bytes 811016 | tf_op jit(solution)/shard_map/ppermute | solution.py:381
  38.2 7.8 %all-to-all-done.1.near = f32[16,16,128]{2,1,0:T(8,128)S(1)} async-done(((f32[16,16,128]{2,1,0:T(8,128)}), f32[16,16,128]{2,1,0:T(8,128)S(1)}, u32[]{:S(2)}, u32[]{:S(2)}) %all-to-all-start.1) | async-done | bytes 131104 | tf_op jit(solution)/shard_map/all_to_all | solution.py:392
  46.0 0.0 collective-permute-start.1
  46.0 0.0 collective-permute-done.8.from_x
  46.1 0.7 collective-permute-start.10
  46.8 0.6 collective-permute-done.1.far
  47.4 4.4 %collective-permute-done.4.diag_re = f32[48,1408]{1,0:T(8,128)S(1)} collective-permute-done((f32[48,1408]{1,0:T(8,128)}, f32[48,1408]{1,0:T(8,128)S(1)}, u32[]{:S(2)}, u32[]{:S(2)}) %collective-permute-start.4) | collective-permute-done | bytes 270368 | tf_op jit(solution)/shard_map/ppermute | solution.py:381
  51.8 0.0 collective-permute-done.5.diag_im
  51.8 0.0 copy-done.2
  51.8 3.2 %shard_map.58 = (f32[48,128]{1,0:T(8,128)S(1)}, f32[16,2,48,128]{3,2,1,0:T(8,128)S(1)}, f32[4,2,48,640]{3,2,1,0:T(8,128)S(1)}) custom-call(f32[16,16,128]{2,1,0:T(8,128)S(1)} %all-to-all-done.1.near, f32[16,16,128]{2,1,0:T(8,128)S(1)} %collective-permute-done.1.far, s32[1,1344]{1,0:T(1,128)S(1)} %copy-done.2, f32[2,48,1408]{2,1,0:T(8,128)S(1)} %shard_map.57.own, ...), custom_call_target="tpu_custom_call" | custom-call | tf_op jit(solution)/shard_map/pallas_call | solution.py:356
  55.0 0.1 collective-permute-start.6
  55.1 0.5 collective-permute-start.14
  55.6 0.0 collective-permute-done.9.from_y
  55.6 1.6 %collective-permute-start.11 = (f32[48,1152]{1,0:T(8,128)S(1)}, f32[48,1152]{1,0:T(8,128)S(1)}, u32[]{:S(2)}, u32[]{:S(2)}) collective-permute-start(f32[48,1152]{1,0:T(8,128)S(1)} %slice_bitcast_fusion.2), channel_id=1, source_target_pairs={{0,2},{1,3},{2,0},{3,1},{4,6},{5,7},{6,4},{7,5},{8,10},{9,11},{10,... | collective-permute-start | bytes 663560 | tf_op jit(solution)/shard_map/ppermute | solution.py:381
  57.2 0.0 collective-permute-done.6
  57.3 1.6 %collective-permute-start.7 = (f32[2,48,128]{2,1,0:T(8,128)S(1)}, f32[2,48,128]{2,1,0:T(8,128)S(1)}, u32[]{:S(2)}, u32[]{:S(2)}) collective-permute-start(f32[2,48,128]{2,1,0:T(8,128)S(1)} %pad_maximum_fusion.2), channel_id=1, source_target_pairs={{0,8},{1,9},{2,10},{3,11},{4,12},{5,13},{6,14},{7,15},{8,0},{9,1},... | collective-permute-start | bytes 147464 | tf_op jit(solution)/shard_map/ppermute | solution.py:381
  58.9 2.5 %collective-permute-done.7 = f32[2,48,128]{2,1,0:T(8,128)S(1)} collective-permute-done((f32[2,48,128]{2,1,0:T(8,128)S(1)}, f32[2,48,128]{2,1,0:T(8,128)S(1)}, u32[]{:S(2)}, u32[]{:S(2)}) %collective-permute-start.7) | collective-permute-done | bytes 49184 | tf_op jit(solution)/shard_map/ppermute | solution.py:381
  61.4 0.0 copy-start.3
  61.4 0.0 collective-permute-done.10.diag_re
  61.4 1.6 %collective-permute-done.11.diag_im = f32[48,1152]{1,0:T(8,128)S(1)} collective-permute-done((f32[48,1152]{1,0:T(8,128)S(1)}, f32[48,1152]{1,0:T(8,128)S(1)}, u32[]{:S(2)}, u32[]{:S(2)}) %collective-permute-start.11) | collective-permute-done | bytes 221216 | tf_op jit(solution)/shard_map/ppermute | solution.py:381
  63.1 1.1 %shard_map.59 = (f32[48,128]{1,0:T(8,128)S(1)}, f32[4,2,48,384]{3,2,1,0:T(8,128)S(1)}) custom-call(f32[4,48,128]{2,1,0:T(8,128)S(1)} %pad_maximum_fusion.wires, f32[2,48,1152]{2,1,0:T(8,128)S(1)} %slice.24.own, f32[2,48,1152]{2,1,0:T(8,128)S(1)} %collective-permute-done.8.from_x, f32[2,48,1152]{2,1,0:T(8,128)S(1)} %collective-permute-done.9.from_y, ...), custom_call_target="tpu_custom_call" | custom-call | tf_op jit(solution)/shard_map/pallas_call | solution.py:356
  64.2 0.1 collective-permute-start.15
  64.2 0.5 collective-permute-start.12
  64.7 1.5 %collective-permute-done.12 = f32[1,48,128]{2,1,0:T(8,128)S(1)} collective-permute-done((f32[1,48,128]{2,1,0:T(8,128)S(1)}, f32[1,48,128]{2,1,0:T(8,128)S(1)}, u32[]{:S(2)}, u32[]{:S(2)}) %collective-permute-start.12) | collective-permute-done | bytes 24608 | tf_op jit(solution)/shard_map/ppermute | solution.py:381
  66.3 1.6 %collective-permute-start.13 = (f32[2,48,128]{2,1,0:T(8,128)S(1)}, f32[2,48,128]{2,1,0:T(8,128)S(1)}, u32[]{:S(2)}, u32[]{:S(2)}) collective-permute-start(f32[2,48,128]{2,1,0:T(8,128)S(1)} %pad_maximum_fusion.3), channel_id=1, source_target_pairs={{0,8},{1,9},{2,10},{3,11},{4,12},{5,13},{6,14},{7,15},{8,0},{9,1},... | collective-permute-start | bytes 147464 | tf_op jit(solution)/shard_map/ppermute | solution.py:381
  67.9 0.9 %slice.27.diag_last = f32[2,48,192]{2,1,0:T(8,128)S(1)} slice(f32[2,48,2880]{2,1,0:T(8,128)} %param.6), slice={[0:2], [0:48], [2688:2880]} | slice | bytes 147456 | tf_op jit(solution)/shard_map/slice | solution.py:406
  68.8 1.6 %collective-permute-done.13 = f32[2,48,128]{2,1,0:T(8,128)S(1)} collective-permute-done((f32[2,48,128]{2,1,0:T(8,128)S(1)}, f32[2,48,128]{2,1,0:T(8,128)S(1)}, u32[]{:S(2)}, u32[]{:S(2)}) %collective-permute-start.13) | collective-permute-done | bytes 49184 | tf_op jit(solution)/shard_map/ppermute | solution.py:381
  70.4 0.0 collective-permute-done.15.diag_far
  70.4 0.0 collective-permute-done.14.couple_far
  70.4 0.0 copy-done.3
  70.4 4.7 %shard_map.60 = f32[16,3,128]{2,1,0:T(4,128)S(1)} custom-call(f32[1536,128]{1,0:T(8,128)S(1)} %bitcast.12, f32[4,48,128]{2,1,0:T(8,128)S(1)} %pad_maximum_fusion.1.wires, s32[1,1344]{1,0:T(1,128)S(1)} %copy-done.2, s32[1,192]{1,0:T(1,128)S(1)} %copy-done.3, f32[4,2,48,640]{3,2,1,0:T(8,128)S(1)} %get-tuple-element.17.couple, ...), custom_call_target="tpu_custom_call" | custom-call | tf_op jit(solution)/shard_map/pallas_call | solution.py:356
  75.1 13.2 %all_to_all.16.received = f32[16,3,128]{2,1,0:T(4,128)S(1)} all-to-all(f32[16,3,128]{2,1,0:T(4,128)S(1)} %shard_map.60), channel_id=1, replica_groups=mesh['leaf'=16,'sub'=2] {'leaf'}, dimensions={0} | all-to-all | bytes 49152 | tf_op jit(solution)/shard_map/all_to_all | solution.py:466
  88.3 0.8 shard_map.61
  (8 shorter events, 0.1 us)
Async XLA Ops:
  0.0 0.8 copy-start.1
  1.0 1.1 %copy-start = (f32[2,48,1344]{2,1,0:T(8,128)S(1)}, f32[2,48,1344]{2,1,0:T(8,128)}, u32[]{:S(2)}) copy-start(f32[2,48,1344]{2,1,0:T(8,128)} %coupling.1) | copy-start | bytes 1548292
  2.1 18.6 %copy-start.4 = (f32[2,48,2880]{2,1,0:T(8,128)S(1)}, f32[2,48,2880]{2,1,0:T(8,128)}, u32[]{:S(2)}) copy-start(f32[2,48,2880]{2,1,0:T(8,128)} %param.6) | copy-start | bytes 3317764
  2.2 28.4 %collective-permute-start.2 = (f32[2,48,1408]{2,1,0:T(8,128)S(1)}, f32[2,48,1408]{2,1,0:T(8,128)S(1)}, u32[]{:S(2)}, u32[]{:S(2)}) collective-permute-start(f32[2,48,1408]{2,1,0:T(8,128)S(1)} %shard_map.57.own), channel_id=1, source_target_pairs={{0,2},{1,3},{2,0},{3,1},{4,6},{5,7},{6,4},{7,5},{8,10},{9,11},{10,... | collective-permute-start | bytes 1622024 | tf_op jit(solution)/shard_map/ppermute | solution.py:381
  20.0 3.8 %collective-permute-start = (f32[16,16,128]{2,1,0:T(8,128)S(1)}, f32[16,16,128]{2,1,0:T(8,128)S(1)}, u32[]{:S(2)}, u32[]{:S(2)}) collective-permute-start(f32[16,16,128]{2,1,0:T(8,128)S(1)} %all_to_all.15.near), channel_id=1, source_target_pairs={{0,1},{1,0},{2,3},{3,2},{4,5},{5,4},{6,7},{7,6},{8,9},{9,8},{10,11... | collective-permute-start | bytes 393224 | tf_op jit(solution)/shard_map/ppermute | solution.py:381
  20.0 15.7 %collective-permute-start.3 = (f32[2,48,1408]{2,1,0:T(8,128)S(1)}, f32[2,48,1408]{2,1,0:T(8,128)S(1)}, u32[]{:S(2)}, u32[]{:S(2)}) collective-permute-start(f32[2,48,1408]{2,1,0:T(8,128)S(1)} %shard_map.57.own), channel_id=1, source_target_pairs={{0,4},{1,5},{2,6},{3,7},{4,0},{5,1},{6,2},{7,3},{8,12},{9,13},{10,... | collective-permute-start | bytes 1622024 | tf_op jit(solution)/shard_map/ppermute | solution.py:381
  20.7 25.4 %collective-permute-start.8 = (f32[2,48,1152]{2,1,0:T(8,128)S(1)}, f32[2,48,1152]{2,1,0:T(8,128)S(1)}, u32[]{:S(2)}, u32[]{:S(2)}) collective-permute-start(f32[2,48,1152]{2,1,0:T(8,128)S(1)} %slice.24.own), channel_id=1, source_target_pairs={{0,2},{1,3},{2,0},{3,1},{4,6},{5,7},{6,4},{7,5},{8,10},{9,11},{10,... | collective-permute-start | bytes 1327112 | tf_op jit(solution)/shard_map/ppermute | solution.py:381
  22.2 33.4 %collective-permute-start.9 = (f32[2,48,1152]{2,1,0:T(8,128)S(1)}, f32[2,48,1152]{2,1,0:T(8,128)S(1)}, u32[]{:S(2)}, u32[]{:S(2)}) collective-permute-start(f32[2,48,1152]{2,1,0:T(8,128)S(1)} %slice.24.own), channel_id=1, source_target_pairs={{0,4},{1,5},{2,6},{3,7},{4,0},{5,1},{6,2},{7,3},{8,12},{9,13},{10,... | collective-permute-start | bytes 1327112 | tf_op jit(solution)/shard_map/ppermute | solution.py:381
  25.5 26.3 %copy-start.2 = (s32[1,1344]{1,0:T(1,128)S(1)}, s32[1,1344]{1,0:T(1,128)}, u32[]{:S(2)}) copy-start(s32[1,1344]{1,0:T(1,128)} %index.3) | copy-start | bytes 16132
  25.5 20.5 %all-to-all-start.1 = ((f32[16,16,128]{2,1,0:T(8,128)}), f32[16,16,128]{2,1,0:T(8,128)S(1)}, u32[]{:S(2)}, u32[]{:S(2)}) async-start(f32[16,16,128]{2,1,0:T(8,128)} %shard_map.56), calls=%async_computation.1 | async-start | bytes 262144 | tf_op jit(solution)/shard_map/all_to_all | solution.py:392
  31.3 20.5 %collective-permute-start.4 = (f32[48,1408]{1,0:T(8,128)}, f32[48,1408]{1,0:T(8,128)S(1)}, u32[]{:S(2)}, u32[]{:S(2)}) collective-permute-start(f32[48,1408]{1,0:T(8,128)} %slice_bitcast_fusion.1), channel_id=1, source_target_pairs={{0,4},{1,5},{2,6},{3,7},{4,0},{5,1},{6,2},{7,3},{8,12},{9,13},{10,... | collective-permute-start | bytes 811016 | tf_op jit(solution)/shard_map/ppermute | solution.py:381
  36.4 15.4 %collective-permute-start.5 = (f32[48,1408]{1,0:T(8,128)}, f32[48,1408]{1,0:T(8,128)}, u32[]{:S(2)}, u32[]{:S(2)}) collective-permute-start(f32[48,1408]{1,0:T(8,128)} %slice_bitcast_fusion), channel_id=1, source_target_pairs={{0,2},{1,3},{2,0},{3,1},{4,6},{5,7},{6,4},{7,5},{8,10},{9,11},{10,... | collective-permute-start | bytes 811016 | tf_op jit(solution)/shard_map/ppermute | solution.py:381
  46.0 1.3 %collective-permute-start.1 = (f32[16,16,128]{2,1,0:T(8,128)S(1)}, f32[16,16,128]{2,1,0:T(8,128)S(1)}, u32[]{:S(2)}, u32[]{:S(2)}) collective-permute-start(f32[16,16,128]{2,1,0:T(8,128)S(1)} %all-to-all-done.1.near), channel_id=1, source_target_pairs={{0,1},{1,0},{2,3},{3,2},{4,5},{5,4},{6,7},{7,6},{8,9},{9,8},{10,11... | collective-permute-start | bytes 393224 | tf_op jit(solution)/shard_map/ppermute | solution.py:381
  46.1 15.4 %collective-permute-start.10 = (f32[48,1152]{1,0:T(8,128)S(1)}, f32[48,1152]{1,0:T(8,128)S(1)}, u32[]{:S(2)}, u32[]{:S(2)}) collective-permute-start(f32[48,1152]{1,0:T(8,128)S(1)} %slice_bitcast_fusion.3), channel_id=1, source_target_pairs={{0,4},{1,5},{2,6},{3,7},{4,0},{5,1},{6,2},{7,3},{8,12},{9,13},{10,... | collective-permute-start | bytes 663560 | tf_op jit(solution)/shard_map/ppermute | solution.py:381
  55.0 2.2 %collective-permute-start.6 = (f32[1,48,128]{2,1,0:T(8,128)S(1)}, f32[1,48,128]{2,1,0:T(8,128)S(1)}, u32[]{:S(2)}, u32[]{:S(2)}) collective-permute-start(f32[1,48,128]{2,1,0:T(8,128)S(1)} %bitcast.13), channel_id=1, source_target_pairs={{0,1},{1,0},{2,3},{3,2},{4,5},{5,4},{6,7},{7,6},{8,9},{9,8},{10,11... | collective-permute-start | bytes 73736 | tf_op jit(solution)/shard_map/ppermute | solution.py:381
  55.1 15.3 %collective-permute-start.14 = (f32[4,2,48,640]{3,2,1,0:T(8,128)S(1)}, f32[4,2,48,640]{3,2,1,0:T(8,128)S(1)}, u32[]{:S(2)}, u32[]{:S(2)}) collective-permute-start(f32[4,2,48,640]{3,2,1,0:T(8,128)S(1)} %get-tuple-element.17.couple), channel_id=1, source_target_pairs={{0,1},{1,0},{2,3},{3,2},{4,5},{5,4},{6,7},{7,6},{8,9},{9,8},{10,11... | collective-permute-start | bytes 2949128 | tf_op jit(solution)/shard_map/ppermute | solution.py:381
  55.6 7.5 %collective-permute-start.11 = (f32[48,1152]{1,0:T(8,128)S(1)}, f32[48,1152]{1,0:T(8,128)S(1)}, u32[]{:S(2)}, u32[]{:S(2)}) collective-permute-start(f32[48,1152]{1,0:T(8,128)S(1)} %slice_bitcast_fusion.2), channel_id=1, source_target_pairs={{0,2},{1,3},{2,0},{3,1},{4,6},{5,7},{6,4},{7,5},{8,10},{9,11},{10,... | collective-permute-start | bytes 663560 | tf_op jit(solution)/shard_map/ppermute | solution.py:381
  57.3 4.2 %collective-permute-start.7 = (f32[2,48,128]{2,1,0:T(8,128)S(1)}, f32[2,48,128]{2,1,0:T(8,128)S(1)}, u32[]{:S(2)}, u32[]{:S(2)}) collective-permute-start(f32[2,48,128]{2,1,0:T(8,128)S(1)} %pad_maximum_fusion.2), channel_id=1, source_target_pairs={{0,8},{1,9},{2,10},{3,11},{4,12},{5,13},{6,14},{7,15},{8,0},{9,1},... | collective-permute-start | bytes 147464 | tf_op jit(solution)/shard_map/ppermute | solution.py:381
  61.4 9.0 %copy-start.3 = (s32[1,192]{1,0:T(1,128)S(1)}, s32[1,192]{1,0:T(1,128)}, u32[]{:S(2)}) copy-start(s32[1,192]{1,0:T(1,128)} %row_map.1) | copy-start | bytes 2308
  64.2 6.2 %collective-permute-start.15 = (f32[4,2,48,384]{3,2,1,0:T(8,128)S(1)}, f32[4,2,48,384]{3,2,1,0:T(8,128)S(1)}, u32[]{:S(2)}, u32[]{:S(2)}) collective-permute-start(f32[4,2,48,384]{3,2,1,0:T(8,128)S(1)} %get-tuple-element.18.diag), channel_id=1, source_target_pairs={{0,1},{1,0},{2,3},{3,2},{4,5},{5,4},{6,7},{7,6},{8,9},{9,8},{10,11... | collective-permute-start | bytes 1769480 | tf_op jit(solution)/shard_map/ppermute | solution.py:381
  64.2 2.0 %collective-permute-start.12 = (f32[1,48,128]{2,1,0:T(8,128)S(1)}, f32[1,48,128]{2,1,0:T(8,128)S(1)}, u32[]{:S(2)}, u32[]{:S(2)}) collective-permute-start(f32[1,48,128]{2,1,0:T(8,128)S(1)} %bitcast.16), channel_id=1, source_target_pairs={{0,1},{1,0},{2,3},{3,2},{4,5},{5,4},{6,7},{7,6},{8,9},{9,8},{10,11... | collective-permute-start | bytes 73736 | tf_op jit(solution)/shard_map/ppermute | solution.py:381
  66.3 4.1 %collective-permute-start.13 = (f32[2,48,128]{2,1,0:T(8,128)S(1)}, f32[2,48,128]{2,1,0:T(8,128)S(1)}, u32[]{:S(2)}, u32[]{:S(2)}) collective-permute-start(f32[2,48,128]{2,1,0:T(8,128)S(1)} %pad_maximum_fusion.3), channel_id=1, source_target_pairs={{0,8},{1,9},{2,10},{3,11},{4,12},{5,13},{6,14},{7,15},{8,0},{9,1},... | collective-permute-start | bytes 147464 | tf_op jit(solution)/shard_map/ppermute | solution.py:381
where the time goes:
time: 89.6 us; the launch traced here: 89.1 us
  blocking collectives  28 us (31%)
  waiting for transfers between devices  22.6 us (25%)
  starting transfers between devices  22.3 us (25%)
  Pallas kernels  11.8 us (13%)
  local copies, waits for them, and re-layouts  4.35 us (5%)
    ppermute x16, starting transfers between devices, hop(): return lax.ppermute(array, AXES, route)  17.2 us
    all_to_all x1, blocking collectives, to_all(): near = lax.all_to_all(wire, 'leaf', 0, 0)  14.8 us
    ppermute x16, waiting for transfers between devices, hop(): return lax.ppermute(array, AXES, route)  14.8 us
    all_to_all x1, blocking collectives, local(): received = lax.all_to_all(packed, 'leaf', 0, 0)  13.2 us
    pallas_call x7, Pallas kernels, call(): pl.pallas_call(functools.partial(kernel, plan, *static), out_shape=shapes...  11.8 us
    all_to_all x1, waiting for transfers between devices, to_all(): near = lax.all_to_all(wire, 'leaf', 0, 0)  7.79 us
    all_to_all x1, starting transfers between devices, to_all(): near = lax.all_to_all(wire, 'leaf', 0, 0)  5.12 us
    unnamed x10, local copies, waits for them, and re-layouts  1.91 us
  transfers between devices with their start and end apart: 17, of which 8 were waited for; matrix products, arithmetic and copies ran while one was open for 3% of the time, Pallas kernels for 7%

commit v1 on v0

--- a/solution.py
+++ b/solution.py
@@ -89,9 +89,10 @@
 
 def spread(wires, target, base, local, flips, lanes_flips, rows, width):
     for entry, flip in enumerate(flips):
+        wire = wires[entry][...]
         for lane_block, lane_flip in enumerate(lanes_flips):
             place = pl.multiple_of(base + (local ^ (flip ^ lane_flip)) * rows, 8)
-            target[pl.ds(place, rows), :] = roll_left(wires[entry], lane_block * width)
+            target[pl.ds(place, rows), :] = roll_left(wire, lane_block * width)
 
 
 class Plan:
@@ -131,28 +132,32 @@
     return scratch[...].T
 
 
-def rhs_kernel(plan, rhs, wire, late, scratch):
-    rows = plan.rows
+def start_kernel(plan, rhs, coupling, wire, joined, scratch):
     first = jnp.concatenate([rhs[0, 0], rhs[1, 0]], axis=0)
     first = transposed(first, scratch)
     padded = plan.groups * plan.group_rows
     blocks = [first[at : at + plan.group_rows] for at in range(0, padded, plan.group_rows)]
     packed = side_by_side(blocks, plan.width)
     wire[...] = jnp.broadcast_to(packed[None], wire.shape)
-    for part in range(2):
-        later = jnp.concatenate([rhs[part, level] for level in range(1, LEVELS)], axis=0)
-        late[part] = transposed(later, scratch)[0:rows]
-
-
-def coupling_kernel(plan, coupling, late, joined):
     whole = plan.couple // LANES * LANES
     tail = plan.couple - whole
     shift = plan.rhs_at % LANES
     for part in range(2):
+        later = jnp.concatenate([rhs[part, level] for level in range(1, LEVELS)], axis=0)
+        later = transposed(later, scratch)[0 : plan.rows]
         joined[part, :, 0:whole] = coupling[part, :, 0:whole]
-        joined[part, :, plan.couple_wide - LANES :] = roll_right(late[part], shift)
+        joined[part, :, plan.couple_wide - LANES :] = roll_right(later, shift)
         if tail:
             joined[part, :, whole : whole + tail] = coupling[part, :, whole : whole + tail]
+
+
+def cut_kernel(plan, diag, middle):
+    middle[...] = diag[:, :, plan.order[0] : sum(plan.order[:-1])]
+
+
+def relay_kernel(plan, from_x, from_y, real, imag):
+    real[...] = from_x[0]
+    imag[...] = from_y[1]
 
 
 def rhs_rows(plan, real, imag, level, shift_cols):
@@ -187,7 +192,8 @@
 def top_kernel(plan, near, far, diag, wire, vector):
     unpack_all(plan, near, far, vector)
     packed = weights(vector[...].reshape(plan.order[0], LANES), plan.width)
-    pack_all(plan, product(diag[0], diag[1], packed, plan.width), wire)
+    top = plan.order[0]
+    pack_all(plan, product(diag[0, :, 0:top], diag[1, :, 0:top], packed, plan.width), wire)
 
 
 def reduce_rows(plan, level, blocks, packed_first_col, packed):
@@ -220,7 +226,9 @@
         rest[at, 1] = imag[:, plan.order[1] :]
 
 
-def first_solve_kernel(plan, flips, wires, own, from_x, from_y, diag_re, diag_im, wire, rest, vector):
+def first_solve_kernel(plan, flips, *refs):
+    wires, refs = refs[: len(flips)], refs[len(flips) :]
+    own, from_x, from_y, diag_re, diag_im, wire, rest, vector = refs
     order = plan.order[1]
     spread(wires, vector, 0, plan.local(1), flips, plan.shared(1), plan.rows, plan.width)
     packed = weights(vector[...], plan.width)
@@ -264,10 +272,15 @@
     return vector[pl.ds(place, plan.rows), :]
 
 
-def tail_kernel(
-    plan, flips, top, wires, index, row_map, couple, couple_far, diag, diag_far, diag_last,
-    out, vector, bounds, front, local_rows, packing,
-):
+def last_diag(plan, diag):
+    start = sum(plan.order[:-1])
+    return diag[0, :, start:], diag[1, :, start:]
+
+
+def tail_kernel(plan, flips, *refs):
+    wires, refs = refs[: len(flips)], refs[len(flips) :]
+    top, index, row_map, couple, couple_far, diag, diag_far, diag_own = refs[:8]
+    out, vector, bounds, front, local_rows, packing = refs[8:]
     rows, width = plan.rows, plan.width
     vector[0 : plan.order[0], :] = top[...]
     spread(wires, vector, plan.order[0], plan.local(1), flips, plan.shared(1), rows, width)
@@ -297,13 +310,15 @@
                 place = pl.multiple_of(base + (local ^ flip) * rows, 8)
                 vector[pl.ds(place, rows), :] = solved
         else:
-            local_rows[level * rows :, :] = product(diag_last[0], diag_last[1], packed, width)
+            local_rows[level * rows :, :] = product(*last_diag(plan, diag_own), packed, width)
     for level in range(LEVELS - 1):
         local_rows[level * rows : (level + 1) * rows, :] = own_rows(plan, vector, level)
     pack_owners(plan, row_map, local_rows, packing, out)
 
 
-def reduce_kernel(plan, level, flips, top, wires, index, couple, wire, vector, bounds):
+def reduce_kernel(plan, level, flips, *refs):
+    wires, refs = refs[: len(flips)], refs[len(flips) :]
+    top, index, couple, wire, vector, bounds = refs
     rows, width = plan.rows, plan.width
     vector[0 : plan.ancestors[level - 1], :] = top[...]
     spread(
@@ -316,7 +331,9 @@
     wire[...] = side_by_side(reduce_rows(plan, level, blocks, plan.order[1], packed), width)
 
 
-def solve_kernel(plan, level, flips, first_col, wires, diag, wire, vector):
+def solve_kernel(plan, level, flips, first_col, *refs):
+    wires, refs = refs[: len(flips)], refs[len(flips) :]
+    diag, wire, vector = refs
     spread(wires, vector, 0, plan.local(level), flips, plan.shared(level), plan.rows, plan.width)
     packed = weights(vector[...], plan.width)
     cols = slice(first_col, first_col + plan.order[level])
@@ -327,12 +344,14 @@
     wire[...] = side_by_side(solved, plan.width)
 
 
-def last_kernel(plan, flips, top, wires, row_map, diag_last, out, front, local_rows, packing):
+def last_kernel(plan, flips, *refs):
+    wires, refs = refs[: len(flips)], refs[len(flips) :]
+    top, row_map, diag_own, out, front, local_rows, packing = refs
     level = LEVELS - 1
     rows, width = plan.rows, plan.width
     spread(wires, front, 0, plan.local(level), flips, plan.shared(level), rows, width)
     packed = weights(front[...], width)
-    local_rows[level * rows :, :] = product(diag_last[0], diag_last[1], packed, width)
+    local_rows[level * rows :, :] = product(*last_diag(plan, diag_own), packed, width)
     for upper in range(level):
         local_rows[upper * rows : (upper + 1) * rows, :] = own_rows(plan, top, upper)
     pack_owners(plan, row_map, local_rows, packing, out)
@@ -376,42 +395,43 @@
     whole_shape = (leafs, total // leafs, rows, LANES)
     block = (rows, LANES)
 
-    def hop(array, bit):
-        route = [(device, device ^ (1 << bit)) for device in range(total)]
+    def flip_to(array, flip):
+        route = [(device, device ^ flip) for device in range(total)]
         return lax.ppermute(array, AXES, route)
 
     def exchange(wire, level):
-        current, flips = wire[None], [0]
-        for bit in plan.open_bits(level):
-            found = hop(current, bit)
-            current = jnp.concatenate([current, found], axis=0)
+        bits = plan.open_bits(level)
+        flips = [0]
+        for bit in bits:
             flips = flips + [flip ^ (1 << bit) for flip in flips]
-        return current, flips
+        if len(bits) <= 2:
+            return [wire] + [flip_to(wire, flip) for flip in flips[1:]], flips
+        current = wire[None]
+        for bit in bits:
+            current = jnp.concatenate([current, flip_to(current, 1 << bit)], axis=0)
+        return [current[at] for at in range(len(flips))], flips
 
     def to_all(wire):
         near = lax.all_to_all(wire, "leaf", 0, 0)
-        return near, hop(near, 0)
+        return near, flip_to(near, 1)
 
     def neighbours(array):
-        return array, hop(array, 1), hop(array, 2)
+        return array, flip_to(array, 2), flip_to(array, 4)
 
     def beyond(pieces):
         own, from_x, from_y = pieces
-        real = hop(from_x[0], 2)
-        return (own, from_x, from_y, real, hop(from_y[1], 1))
-
-    diag_top = diag_inverse[:, :, : order[0]]
-    middle = sum(order[:-1])
-    diag_mid = diag_inverse[:, :, order[0] : middle]
-    diag_last = diag_inverse[:, :, middle:]
-
-    wire, late = call(
-        rhs_kernel, plan, [wire_shape, (2, rows, LANES)], [(LANES, LANES)], [right_sides]
-    )
-    (joined,) = call(coupling_kernel, plan, [(2, rows, plan.couple_wide)], [], [coupling, late])
+        real, imag = call(relay_kernel, plan, [own.shape[1:]] * 2, [], [from_x, from_y])
+        real, imag = flip_to(real, 4), flip_to(imag, 2)
+        return own, from_x, from_y, real, imag
+
+    wire, joined = call(
+        start_kernel, plan, [wire_shape, (2, rows, plan.couple_wide)], [(LANES, LANES)],
+        [right_sides, coupling],
+    )
+    (diag_mid,) = call(cut_kernel, plan, [(2, rows, sum(order[1:-1]))], [], [diag_inverse])
     gathered = to_all(wire)
     couple = beyond(neighbours(joined))
-    (wire,) = call(top_kernel, plan, [wire_shape], [whole_shape], [*gathered, diag_top])
+    (wire,) = call(top_kernel, plan, [wire_shape], [whole_shape], [*gathered, diag_inverse])
     gathered = to_all(wire)
     diag = beyond(neighbours(diag_mid))
     wire, top, couple_rest = call(
@@ -424,12 +444,12 @@
     wires, flips = exchange(wire, 1)
     wire, diag_rest = call(
         first_solve_kernel, plan, [block, (4, 2, rows, diag_mid.shape[2] - order[1])],
-        [(order[1], LANES)], [wires, *diag], static=(flips,),
+        [(order[1], LANES)], [*wires, *diag], static=(flips,),
     )
     wires, flips = exchange(wire, 1)
     if plan.members[2] <= 8:
-        couple_far = hop(couple_rest, 0)
-        diag_far = hop(diag_rest, 0)
+        couple_far = flip_to(couple_rest, 1)
+        diag_far = flip_to(diag_rest, 1)
         (packed,) = call(
             tail_kernel, plan, [(leafs, owner_rows, LANES)],
             [
@@ -437,10 +457,10 @@
                 (LEVELS * rows, LANES), packing,
             ],
             [
-                top, wires, boundary, plane_map, couple_rest, couple_far, diag_rest, diag_far,
-                diag_last,
+                *wires, top, boundary, plane_map, couple_rest, couple_far, diag_rest, diag_far,
+                diag_inverse,
             ],
-            scalars=(2, 3), static=(flips,),
+            scalars=(len(flips) + 1, len(flips) + 2), static=(flips,),
         )
     else:
         first_col = 0
@@ -448,20 +468,21 @@
             wire, top = call(
                 reduce_kernel, plan, [block, (plan.ancestors[level], LANES)],
                 [(order[level], LANES)],
-                [top, wires, boundary, couple_rest], scalars=(2,), static=(level, flips),
+                [*wires, top, boundary, couple_rest], scalars=(len(flips) + 1,),
+                static=(level, flips),
             )
             wires, flips = exchange(wire, level)
             if level + 1 < LEVELS:
                 (wire,) = call(
                     solve_kernel, plan, [block], [(order[level], LANES)],
-                    [wires, diag_rest], static=(level, flips, first_col),
+                    [*wires, diag_rest], static=(level, flips, first_col),
                 )
                 first_col += order[level]
                 wires, flips = exchange(wire, level)
         (packed,) = call(
             last_kernel, plan, [(leafs, owner_rows, LANES)],
             [(order[-1], LANES), (LEVELS * rows, LANES), packing],
-            [top, wires, plane_map, diag_last], scalars=(2,), static=(flips,),
+            [*wires, top, plane_map, diag_inverse], scalars=(len(flips) + 1,), static=(flips,),
         )
     received = lax.all_to_all(packed, "leaf", 0, 0)
     (field,) = call(

time: 89.6 us -> 90.9 us (1.015)
  waiting for transfers between devices: 22.6 us -> 27 us
  blocking collectives: 28 us -> 25.6 us
  Pallas kernels: 11.8 us -> 13.8 us
  starting transfers between devices: 22.3 us -> 20.8 us
  local copies, waits for them, and re-layouts: 4.35 us -> 3.16 us
    ppermute x16 -> x18, waiting for transfers between devices: 14.8 us -> 24.2 us  [flip_to(): return lax.ppermute(array, AXES, route)]
    all_to_all x1, waiting for transfers between devices: 7.79 us -> 2.81 us  [to_all(): near = lax.all_to_all(wire, 'leaf', 0, 0)]
    ppermute x16 -> x18, starting transfers between devices: 17.2 us -> 14.8 us  [flip_to(): return lax.ppermute(array, AXES, route)]
    pallas_call x7 -> x9, Pallas kernels: 11.8 us -> 13.8 us  [call(): pl.pallas_call(functools.partial(kernel, plan, *static), out_shape=shapes...]
    squeeze x4 -> x0, local copies, waits for them, and re-layouts: 1.48 us -> none  [the longest x2 0.74 us: beyond(): return (own, from_x, from_y, real, hop(from_y[1], 1))]
    all_to_all x1, blocking collectives: 13.2 us -> 11.8 us  [local(): received = lax.all_to_all(packed, 'leaf', 0, 0)]
    unnamed x10 -> x12, local copies, waits for them, and re-layouts: 1.91 us -> 3.16 us
    slice x3 -> x0, local copies, waits for them, and re-layouts: 0.97 us -> none  [the longest x1 0.9 us: local(): diag_last = diag_inverse[:, :, middle:]]
  transfers between devices with their start and end apart: 17 -> 19, of which waited for: 8 -> 10; matrix products, arithmetic and copies ran while one was open for 3% -> 0% of each run, Pallas kernels for 7% -> 8%
where the time goes in v1:
time: 90.9 us; the launch traced here: 90.5 us
  waiting for transfers between devices  27 us (30%)
  blocking collectives  25.6 us (28%)
  starting transfers between devices  20.8 us (23%)
  Pallas kernels  13.8 us (15%)
  local copies, waits for them, and re-layouts  3.16 us (3%)
    ppermute x18, waiting for transfers between devices, flip_to(): return lax.ppermute(array, AXES, route)  24.2 us
    ppermute x18, starting transfers between devices, flip_to(): return lax.ppermute(array, AXES, route)  14.8 us
    all_to_all x1, blocking collectives, to_all(): near = lax.all_to_all(wire, 'leaf', 0, 0)  13.8 us
    pallas_call x9, Pallas kernels, call(): pl.pallas_call(functools.partial(kernel, plan, *static), out_shape=shapes...  13.8 us
    all_to_all x1, blocking collectives, local(): received = lax.all_to_all(packed, 'leaf', 0, 0)  11.8 us
    all_to_all x1, starting transfers between devices, to_all(): near = lax.all_to_all(wire, 'leaf', 0, 0)  5.99 us
    unnamed x12, local copies, waits for them, and re-layouts  3.16 us
    all_to_all x1, waiting for transfers between devices, to_all(): near = lax.all_to_all(wire, 'leaf', 0, 0)  2.81 us
  transfers between devices with their start and end apart: 19, of which 10 were waited for; matrix products, arithmetic and copies ran while one was open for 0% of the time, Pallas kernels for 8%

profile of v1, /device:TPU:0, one launch (start us, length us, event | category | flops | bytes accessed | tf_op | source)
XLA Modules:
  0.0 90.5 jit_solution(6557952159602959275)
XLA Ops:
  0.0 0.0 copy-start.2
  0.0 1.0 %copy-done.2 = f32[2,48,1344]{2,1,0:T(8,128)S(1)} copy-done((f32[2,48,1344]{2,1,0:T(8,128)S(1)}, f32[2,48,1344]{2,1,0:T(8,128)}, u32[]{:S(2)}) %copy-start.2) | copy-done | bytes 516120
  1.0 0.0 copy-start.3
  1.1 0.8 copy-done.3
  1.9 1.0 %shard_map.55 = (f32[16,16,128]{2,1,0:T(8,128)S(1)}, f32[2,48,1408]{2,1,0:T(8,128)}) custom-call(f32[2,4,16,48]{3,2,1,0:T(8,128)S(1)} %copy-done.3, f32[2,48,1344]{2,1,0:T(8,128)S(1)} %copy-done.2), custom_call_target="tpu_custom_call" | custom-call | tf_op jit(solution)/shard_map/pallas_call | solution.py:375
  2.9 3.0 %collective-permute-start.2 = (f32[2,48,1408]{2,1,0:T(8,128)}, f32[2,48,1408]{2,1,0:T(8,128)S(1)}, u32[]{:S(2)}, u32[]{:S(2)}) collective-permute-start(f32[2,48,1408]{2,1,0:T(8,128)} %get-tuple-element.17.own), channel_id=1, source_target_pairs={{0,2},{1,3},{2,0},{3,1},{4,6},{5,7},{6,4},{7,5},{8,10},{9,11},{10,... | collective-permute-start | bytes 1622024 | tf_op jit(solution)/shard_map/ppermute | solution.py:400
  5.9 1.5 %collective-permute-start.3 = (f32[2,48,1408]{2,1,0:T(8,128)}, f32[2,48,1408]{2,1,0:T(8,128)S(1)}, u32[]{:S(2)}, u32[]{:S(2)}) collective-permute-start(f32[2,48,1408]{2,1,0:T(8,128)} %get-tuple-element.17.own), channel_id=1, source_target_pairs={{0,4},{1,5},{2,6},{3,7},{4,0},{5,1},{6,2},{7,3},{8,12},{9,13},{10,... | collective-permute-start | bytes 1622024 | tf_op jit(solution)/shard_map/ppermute | solution.py:400
  7.4 13.8 %all_to_all.15.near = f32[16,16,128]{2,1,0:T(8,128)S(1)} all-to-all(f32[16,16,128]{2,1,0:T(8,128)S(1)} %get-tuple-element.16), channel_id=1, replica_groups=mesh['leaf'=16,'sub'=2] {'leaf'}, dimensions={0} | all-to-all | bytes 262144 | tf_op jit(solution)/shard_map/all_to_all | solution.py:415
  21.2 0.0 collective-permute-start
  21.2 1.3 %collective-permute-done.far = f32[16,16,128]{2,1,0:T(8,128)S(1)} collective-permute-done((f32[16,16,128]{2,1,0:T(8,128)S(1)}, f32[16,16,128]{2,1,0:T(8,128)S(1)}, u32[]{:S(2)}, u32[]{:S(2)}) %collective-permute-start) | collective-permute-done | bytes 131104 | tf_op jit(solution)/shard_map/ppermute | solution.py:400
  22.6 0.0 copy-start
  22.6 1.3 %copy-done = f32[2,48,2880]{2,1,0:T(8,128)S(1)} copy-done((f32[2,48,2880]{2,1,0:T(8,128)S(1)}, f32[2,48,2880]{2,1,0:T(8,128)}, u32[]{:S(2)}) %copy-start) | copy-done | bytes 1105944
  23.8 0.0 copy-start.1
  23.8 1.7 %shard_map.56 = f32[16,16,128]{2,1,0:T(8,128)} custom-call(f32[16,16,128]{2,1,0:T(8,128)S(1)} %all_to_all.15.near, f32[16,16,128]{2,1,0:T(8,128)S(1)} %collective-permute-done.far, f32[2,48,2880]{2,1,0:T(8,128)S(1)} %copy-done), custom_call_target="tpu_custom_call" | custom-call | tf_op jit(solution)/shard_map/pallas_call | solution.py:375
  25.6 6.0 %all-to-all-start.1 = ((f32[16,16,128]{2,1,0:T(8,128)}), f32[16,16,128]{2,1,0:T(8,128)}, u32[]{:S(2)}, u32[]{:S(2)}) async-start(f32[16,16,128]{2,1,0:T(8,128)} %shard_map.56), calls=%async_computation.1 | async-start | bytes 262144 | tf_op jit(solution)/shard_map/all_to_all | solution.py:415
  31.6 0.0 copy-done.1
  31.6 0.0 copy-start.4
  31.6 1.9 %collective-permute-start.10 = (f32[2,48,1152]{2,1,0:T(8,128)S(1)}, f32[2,48,1152]{2,1,0:T(8,128)S(1)}, u32[]{:S(2)}, u32[]{:S(2)}) collective-permute-start(f32[2,48,1152]{2,1,0:T(8,128)S(1)} %shard_map.59.refs_4_), channel_id=1, source_target_pairs={{0,4},{1,5},{2,6},{3,7},{4,0},{5,1},{6,2},{7,3},{8,12},{9,13},{10,... | collective-permute-start | bytes 1327112 | tf_op jit(solution)/shard_map/ppermute | solution.py:400
  33.6 1.5 %collective-permute-start.9 = (f32[2,48,1152]{2,1,0:T(8,128)S(1)}, f32[2,48,1152]{2,1,0:T(8,128)S(1)}, u32[]{:S(2)}, u32[]{:S(2)}) collective-permute-start(f32[2,48,1152]{2,1,0:T(8,128)S(1)} %shard_map.59.refs_4_), channel_id=1, source_target_pairs={{0,2},{1,3},{2,0},{3,1},{4,6},{5,7},{6,4},{7,5},{8,10},{9,11},{10,... | collective-permute-start | bytes 1327112 | tf_op jit(solution)/shard_map/ppermute | solution.py:400
  35.0 0.0 collective-permute-done.2.from_x
  35.0 0.0 collective-permute-done.3.from_y
  35.0 0.9 shard_map.57
  35.9 0.6 collective-permute-start.4
  36.4 0.2 collective-permute-start.5
  36.6 2.8 %all-to-all-done.1.near = f32[16,16,128]{2,1,0:T(8,128)} async-done(((f32[16,16,128]{2,1,0:T(8,128)}), f32[16,16,128]{2,1,0:T(8,128)}, u32[]{:S(2)}, u32[]{:S(2)}) %all-to-all-start.1) | async-done | bytes 131104 | tf_op jit(solution)/shard_map/all_to_all | solution.py:415
  39.4 0.0 collective-permute-start.1
  39.4 1.6 %collective-permute-done.1.far = f32[16,16,128]{2,1,0:T(8,128)S(1)} collective-permute-done((f32[16,16,128]{2,1,0:T(8,128)}, f32[16,16,128]{2,1,0:T(8,128)S(1)}, u32[]{:S(2)}, u32[]{:S(2)}) %collective-permute-start.1) | collective-permute-done | bytes 131104 | tf_op jit(solution)/shard_map/ppermute | solution.py:400
  41.0 9.9 %collective-permute-done.4.diag_re = f32[48,1408]{1,0:T(8,128)} collective-permute-done((f32[48,1408]{1,0:T(8,128)}, f32[48,1408]{1,0:T(8,128)}, u32[]{:S(2)}, u32[]{:S(2)}) %collective-permute-start.4) | collective-permute-done | bytes 270368 | tf_op jit(solution)/shard_map/ppermute | solution.py:400
  50.9 0.9 collective-permute-done.5.diag_im
  51.8 0.0 copy-done.4
  51.8 3.4 %shard_map.58 = (f32[48,128]{1,0:T(8,128)S(1)}, f32[16,2,48,128]{3,2,1,0:T(8,128)S(1)}, f32[4,2,48,640]{3,2,1,0:T(8,128)S(1)}) custom-call(f32[16,16,128]{2,1,0:T(8,128)} %all-to-all-done.1.near, f32[16,16,128]{2,1,0:T(8,128)S(1)} %collective-permute-done.1.far, s32[1,1344]{1,0:T(1,128)S(1)} %copy-done.4, f32[2,48,1408]{2,1,0:T(8,128)} %get-tuple-element.17.own, ...), custom_call_target="tpu_custom_call" | custom-call | tf_op jit(solution)/shard_map/pallas_call | solution.py:375
  55.2 0.1 collective-permute-start.16
  55.3 0.0 collective-permute-done.10.from_y.refs_6_
  55.3 0.0 collective-permute-done.9.from_x.refs_5_
  55.3 0.0 copy-start.5
  55.4 0.8 collective-permute-start.11
  56.2 1.3 %collective-permute-start.12 = (f32[48,1152]{1,0:T(8,128)S(1)}, f32[48,1152]{1,0:T(8,128)S(1)}, u32[]{:S(2)}, u32[]{:S(2)}) collective-permute-start(f32[48,1152]{1,0:T(8,128)S(1)} %get-tuple-element.22), channel_id=1, source_target_pairs={{0,2},{1,3},{2,0},{3,1},{4,6},{5,7},{6,4},{7,5},{8,10},{9,11},{10,... | collective-permute-start | bytes 663560 | tf_op jit(solution)/shard_map/ppermute | solution.py:400
  57.4 0.0 collective-permute-start.6
  57.5 1.4 %collective-permute-start.7 = (f32[48,128]{1,0:T(8,128)S(1)}, f32[48,128]{1,0:T(8,128)S(1)}, u32[]{:S(2)}, u32[]{:S(2)}) collective-permute-start(f32[48,128]{1,0:T(8,128)S(1)} %get-tuple-element.20.refs_0_), channel_id=1, source_target_pairs={{0,8},{1,9},{2,10},{3,11},{4,12},{5,13},{6,14},{7,15},{8,0},{9,1},... | collective-permute-start | bytes 73736 | tf_op jit(solution)/shard_map/ppermute | solution.py:400
  58.9 4.4 %collective-permute-done.11.refs_7_ = f32[48,1152]{1,0:T(8,128)S(1)} collective-permute-done((f32[48,1152]{1,0:T(8,128)S(1)}, f32[48,1152]{1,0:T(8,128)S(1)}, u32[]{:S(2)}, u32[]{:S(2)}) %collective-permute-start.11) | collective-permute-done | bytes 221216 | tf_op jit(solution)/shard_map/ppermute | solution.py:400
  63.2 0.6 collective-permute-start.8
  63.9 0.0 collective-permute-done.12.refs_8_
  63.9 0.0 collective-permute-done.6.refs_1_
  63.9 0.0 collective-permute-done.7.refs_2_
  63.9 2.8 %collective-permute-done.8.refs_3_ = f32[48,128]{1,0:T(8,128)S(1)} collective-permute-done((f32[48,128]{1,0:T(8,128)S(1)}, f32[48,128]{1,0:T(8,128)S(1)}, u32[]{:S(2)}, u32[]{:S(2)}) %collective-permute-start.8) | collective-permute-done | bytes 24608 | tf_op jit(solution)/shard_map/ppermute | solution.py:400
  66.7 1.1 %shard_map.61 = (f32[48,128]{1,0:T(8,128)S(1)}, f32[4,2,48,384]{3,2,1,0:T(8,128)S(1)}) custom-call(f32[48,128]{1,0:T(8,128)S(1)} %get-tuple-element.20.refs_0_, f32[48,128]{1,0:T(8,128)S(1)} %collective-permute-done.6.refs_1_, f32[48,128]{1,0:T(8,128)S(1)} %collective-permute-done.7.refs_2_, f32[48,128]{1,0:T(8,128)S(1)} %collective-permute-done.8.refs_3_, ...), custom_call_target="tpu_custom_call" | custom-call | tf_op jit(solution)/shard_map/pallas_call | solution.py:375
  67.8 0.1 collective-permute-start.17
  68.0 0.4 collective-permute-start.13
  68.4 1.2 %collective-permute-start.14 = (f32[48,128]{1,0:T(8,128)S(1)}, f32[48,128]{1,0:T(8,128)S(1)}, u32[]{:S(2)}, u32[]{:S(2)}) collective-permute-start(f32[48,128]{1,0:T(8,128)S(1)} %get-tuple-element.23.refs_0_), channel_id=1, source_target_pairs={{0,8},{1,9},{2,10},{3,11},{4,12},{5,13},{6,14},{7,15},{8,0},{9,1},... | collective-permute-start | bytes 73736 | tf_op jit(solution)/shard_map/ppermute | solution.py:400
  69.6 0.2 collective-permute-start.15
  69.8 0.1 collective-permute-done.13.refs_1_
  69.9 2.3 %collective-permute-done.14.refs_2_ = f32[48,128]{1,0:T(8,128)S(1)} collective-permute-done((f32[48,128]{1,0:T(8,128)S(1)}, f32[48,128]{1,0:T(8,128)S(1)}, u32[]{:S(2)}, u32[]{:S(2)}) %collective-permute-start.14) | collective-permute-done | bytes 24608 | tf_op jit(solution)/shard_map/ppermute | solution.py:400
  72.2 0.9 %collective-permute-done.15.refs_3_ = f32[48,128]{1,0:T(8,128)S(1)} collective-permute-done((f32[48,128]{1,0:T(8,128)S(1)}, f32[48,128]{1,0:T(8,128)S(1)}, u32[]{:S(2)}, u32[]{:S(2)}) %collective-permute-start.15) | collective-permute-done | bytes 24608 | tf_op jit(solution)/shard_map/ppermute | solution.py:400
  73.1 0.0 collective-permute-done.17.refs_10_
  73.1 0.0 collective-permute-done.16.refs_8_
  73.1 0.0 copy-done.5
  73.1 4.8 %shard_map.62 = f32[16,3,128]{2,1,0:T(4,128)S(1)} custom-call(f32[48,128]{1,0:T(8,128)S(1)} %get-tuple-element.23.refs_0_, f32[48,128]{1,0:T(8,128)S(1)} %collective-permute-done.13.refs_1_, f32[48,128]{1,0:T(8,128)S(1)} %collective-permute-done.14.refs_2_, f32[48,128]{1,0:T(8,128)S(1)} %collective-permute-done.15.refs_3_, f32[1536,128]{1,0:T(8,128)S(1)} %bitcast.2, ...), custom_call_target="tpu_custom_call" | custom-call | tf_op jit(solution)/shard_map/pallas_call | solution.py:375
  77.9 11.8 %all_to_all.16.received = f32[16,3,128]{2,1,0:T(4,128)S(1)} all-to-all(f32[16,3,128]{2,1,0:T(4,128)S(1)} %shard_map.62), channel_id=1, replica_groups=mesh['leaf'=16,'sub'=2] {'leaf'}, dimensions={0} | all-to-all | bytes 49152 | tf_op jit(solution)/shard_map/all_to_all | solution.py:487
  89.7 0.8 shard_map.63
  (2 shorter events, 0.1 us)
Async XLA Ops:
  0.0 1.0 %copy-start.2 = (f32[2,48,1344]{2,1,0:T(8,128)S(1)}, f32[2,48,1344]{2,1,0:T(8,128)}, u32[]{:S(2)}) copy-start(f32[2,48,1344]{2,1,0:T(8,128)} %coupling.1) | copy-start | bytes 1548292
  1.0 0.8 copy-start.3
  2.9 32.1 %collective-permute-start.2 = (f32[2,48,1408]{2,1,0:T(8,128)}, f32[2,48,1408]{2,1,0:T(8,128)S(1)}, u32[]{:S(2)}, u32[]{:S(2)}) collective-permute-start(f32[2,48,1408]{2,1,0:T(8,128)} %get-tuple-element.17.own), channel_id=1, source_target_pairs={{0,2},{1,3},{2,0},{3,1},{4,6},{5,7},{6,4},{7,5},{8,10},{9,11},{10,... | collective-permute-start | bytes 1622024 | tf_op jit(solution)/shard_map/ppermute | solution.py:400
  5.9 29.1 %collective-permute-start.3 = (f32[2,48,1408]{2,1,0:T(8,128)}, f32[2,48,1408]{2,1,0:T(8,128)S(1)}, u32[]{:S(2)}, u32[]{:S(2)}) collective-permute-start(f32[2,48,1408]{2,1,0:T(8,128)} %get-tuple-element.17.own), channel_id=1, source_target_pairs={{0,4},{1,5},{2,6},{3,7},{4,0},{5,1},{6,2},{7,3},{8,12},{9,13},{10,... | collective-permute-start | bytes 1622024 | tf_op jit(solution)/shard_map/ppermute | solution.py:400
  21.2 1.3 %collective-permute-start = (f32[16,16,128]{2,1,0:T(8,128)S(1)}, f32[16,16,128]{2,1,0:T(8,128)S(1)}, u32[]{:S(2)}, u32[]{:S(2)}) collective-permute-start(f32[16,16,128]{2,1,0:T(8,128)S(1)} %all_to_all.15.near), channel_id=1, source_target_pairs={{0,1},{1,0},{2,3},{3,2},{4,5},{5,4},{6,7},{7,6},{8,9},{9,8},{10,11... | collective-permute-start | bytes 393224 | tf_op jit(solution)/shard_map/ppermute | solution.py:400
  22.6 1.3 %copy-start = (f32[2,48,2880]{2,1,0:T(8,128)S(1)}, f32[2,48,2880]{2,1,0:T(8,128)}, u32[]{:S(2)}) copy-start(f32[2,48,2880]{2,1,0:T(8,128)} %refs_11_.1) | copy-start | bytes 3317764
  23.8 7.7 %copy-start.1 = (f32[2,48,2880]{2,1,0:T(8,128)S(1)}, f32[2,48,2880]{2,1,0:T(8,128)}, u32[]{:S(2)}) copy-start(f32[2,48,2880]{2,1,0:T(8,128)} %refs_11_.1) | copy-start | bytes 3317764
  25.6 13.9 %all-to-all-start.1 = ((f32[16,16,128]{2,1,0:T(8,128)}), f32[16,16,128]{2,1,0:T(8,128)}, u32[]{:S(2)}, u32[]{:S(2)}) async-start(f32[16,16,128]{2,1,0:T(8,128)} %shard_map.56), calls=%async_computation.1 | async-start | bytes 262144 | tf_op jit(solution)/shard_map/all_to_all | solution.py:415
  31.6 20.2 %copy-start.4 = (s32[1,1344]{1,0:T(1,128)S(1)}, s32[1,1344]{1,0:T(1,128)}, u32[]{:S(2)}) copy-start(s32[1,1344]{1,0:T(1,128)} %refs_5_.1) | copy-start | bytes 16132
  31.6 23.7 %collective-permute-start.10 = (f32[2,48,1152]{2,1,0:T(8,128)S(1)}, f32[2,48,1152]{2,1,0:T(8,128)S(1)}, u32[]{:S(2)}, u32[]{:S(2)}) collective-permute-start(f32[2,48,1152]{2,1,0:T(8,128)S(1)} %shard_map.59.refs_4_), channel_id=1, source_target_pairs={{0,4},{1,5},{2,6},{3,7},{4,0},{5,1},{6,2},{7,3},{8,12},{9,13},{10,... | collective-permute-start | bytes 1327112 | tf_op jit(solution)/shard_map/ppermute | solution.py:400
  33.6 21.7 %collective-permute-start.9 = (f32[2,48,1152]{2,1,0:T(8,128)S(1)}, f32[2,48,1152]{2,1,0:T(8,128)S(1)}, u32[]{:S(2)}, u32[]{:S(2)}) collective-permute-start(f32[2,48,1152]{2,1,0:T(8,128)S(1)} %shard_map.59.refs_4_), channel_id=1, source_target_pairs={{0,2},{1,3},{2,0},{3,1},{4,6},{5,7},{6,4},{7,5},{8,10},{9,11},{10,... | collective-permute-start | bytes 1327112 | tf_op jit(solution)/shard_map/ppermute | solution.py:400
  35.9 15.0 %collective-permute-start.4 = (f32[48,1408]{1,0:T(8,128)}, f32[48,1408]{1,0:T(8,128)}, u32[]{:S(2)}, u32[]{:S(2)}) collective-permute-start(f32[48,1408]{1,0:T(8,128)} %get-tuple-element.18), channel_id=1, source_target_pairs={{0,4},{1,5},{2,6},{3,7},{4,0},{5,1},{6,2},{7,3},{8,12},{9,13},{10,... | collective-permute-start | bytes 811016 | tf_op jit(solution)/shard_map/ppermute | solution.py:400
  36.4 15.3 %collective-permute-start.5 = (f32[48,1408]{1,0:T(8,128)}, f32[48,1408]{1,0:T(8,128)}, u32[]{:S(2)}, u32[]{:S(2)}) collective-permute-start(f32[48,1408]{1,0:T(8,128)} %get-tuple-element.19), channel_id=1, source_target_pairs={{0,2},{1,3},{2,0},{3,1},{4,6},{5,7},{6,4},{7,5},{8,10},{9,11},{10,... | collective-permute-start | bytes 811016 | tf_op jit(solution)/shard_map/ppermute | solution.py:400
  39.4 1.6 %collective-permute-start.1 = (f32[16,16,128]{2,1,0:T(8,128)}, f32[16,16,128]{2,1,0:T(8,128)S(1)}, u32[]{:S(2)}, u32[]{:S(2)}) collective-permute-start(f32[16,16,128]{2,1,0:T(8,128)} %all-to-all-done.1.near), channel_id=1, source_target_pairs={{0,1},{1,0},{2,3},{3,2},{4,5},{5,4},{6,7},{7,6},{8,9},{9,8},{10,11... | collective-permute-start | bytes 393224 | tf_op jit(solution)/shard_map/ppermute | solution.py:400
  55.2 17.9 %collective-permute-start.16 = (f32[4,2,48,640]{3,2,1,0:T(8,128)S(1)}, f32[4,2,48,640]{3,2,1,0:T(8,128)S(1)}, u32[]{:S(2)}, u32[]{:S(2)}) collective-permute-start(f32[4,2,48,640]{3,2,1,0:T(8,128)S(1)} %get-tuple-element.25.refs_7_), channel_id=1, source_target_pairs={{0,1},{1,0},{2,3},{3,2},{4,5},{5,4},{6,7},{7,6},{8,9},{9,8},{10,11... | collective-permute-start | bytes 2949128 | tf_op jit(solution)/shard_map/ppermute | solution.py:400
  55.3 17.8 %copy-start.5 = (s32[1,192]{1,0:T(1,128)S(1)}, s32[1,192]{1,0:T(1,128)}, u32[]{:S(2)}) copy-start(s32[1,192]{1,0:T(1,128)} %refs_6_.1) | copy-start | bytes 2308
  55.4 7.9 %collective-permute-start.11 = (f32[48,1152]{1,0:T(8,128)S(1)}, f32[48,1152]{1,0:T(8,128)S(1)}, u32[]{:S(2)}, u32[]{:S(2)}) collective-permute-start(f32[48,1152]{1,0:T(8,128)S(1)} %get-tuple-element.21), channel_id=1, source_target_pairs={{0,4},{1,5},{2,6},{3,7},{4,0},{5,1},{6,2},{7,3},{8,12},{9,13},{10,... | collective-permute-start | bytes 663560 | tf_op jit(solution)/shard_map/ppermute | solution.py:400
  56.2 7.7 %collective-permute-start.12 = (f32[48,1152]{1,0:T(8,128)S(1)}, f32[48,1152]{1,0:T(8,128)S(1)}, u32[]{:S(2)}, u32[]{:S(2)}) collective-permute-start(f32[48,1152]{1,0:T(8,128)S(1)} %get-tuple-element.22), channel_id=1, source_target_pairs={{0,2},{1,3},{2,0},{3,1},{4,6},{5,7},{6,4},{7,5},{8,10},{9,11},{10,... | collective-permute-start | bytes 663560 | tf_op jit(solution)/shard_map/ppermute | solution.py:400
  57.4 6.4 %collective-permute-start.6 = (f32[48,128]{1,0:T(8,128)S(1)}, f32[48,128]{1,0:T(8,128)S(1)}, u32[]{:S(2)}, u32[]{:S(2)}) collective-permute-start(f32[48,128]{1,0:T(8,128)S(1)} %get-tuple-element.20.refs_0_), channel_id=1, source_target_pairs={{0,1},{1,0},{2,3},{3,2},{4,5},{5,4},{6,7},{7,6},{8,9},{9,8},{10,11... | collective-permute-start | bytes 73736 | tf_op jit(solution)/shard_map/ppermute | solution.py:400
  57.5 6.4 %collective-permute-start.7 = (f32[48,128]{1,0:T(8,128)S(1)}, f32[48,128]{1,0:T(8,128)S(1)}, u32[]{:S(2)}, u32[]{:S(2)}) collective-permute-start(f32[48,128]{1,0:T(8,128)S(1)} %get-tuple-element.20.refs_0_), channel_id=1, source_target_pairs={{0,8},{1,9},{2,10},{3,11},{4,12},{5,13},{6,14},{7,15},{8,0},{9,1},... | collective-permute-start | bytes 73736 | tf_op jit(solution)/shard_map/ppermute | solution.py:400
  63.2 3.5 %collective-permute-start.8 = (f32[48,128]{1,0:T(8,128)S(1)}, f32[48,128]{1,0:T(8,128)S(1)}, u32[]{:S(2)}, u32[]{:S(2)}) collective-permute-start(f32[48,128]{1,0:T(8,128)S(1)} %get-tuple-element.20.refs_0_), channel_id=1, source_target_pairs={{0,9},{1,8},{2,11},{3,10},{4,13},{5,12},{6,15},{7,14},{8,1},{9,0},... | collective-permute-start | bytes 73736 | tf_op jit(solution)/shard_map/ppermute | solution.py:400
  67.8 5.3 %collective-permute-start.17 = (f32[4,2,48,384]{3,2,1,0:T(8,128)S(1)}, f32[4,2,48,384]{3,2,1,0:T(8,128)S(1)}, u32[]{:S(2)}, u32[]{:S(2)}) collective-permute-start(f32[4,2,48,384]{3,2,1,0:T(8,128)S(1)} %get-tuple-element.26.refs_9_), channel_id=1, source_target_pairs={{0,1},{1,0},{2,3},{3,2},{4,5},{5,4},{6,7},{7,6},{8,9},{9,8},{10,11... | collective-permute-start | bytes 1769480 | tf_op jit(solution)/shard_map/ppermute | solution.py:400
  68.0 2.0 %collective-permute-start.13 = (f32[48,128]{1,0:T(8,128)S(1)}, f32[48,128]{1,0:T(8,128)S(1)}, u32[]{:S(2)}, u32[]{:S(2)}) collective-permute-start(f32[48,128]{1,0:T(8,128)S(1)} %get-tuple-element.23.refs_0_), channel_id=1, source_target_pairs={{0,1},{1,0},{2,3},{3,2},{4,5},{5,4},{6,7},{7,6},{8,9},{9,8},{10,11... | collective-permute-start | bytes 73736 | tf_op jit(solution)/shard_map/ppermute | solution.py:400
  68.4 3.8 %collective-permute-start.14 = (f32[48,128]{1,0:T(8,128)S(1)}, f32[48,128]{1,0:T(8,128)S(1)}, u32[]{:S(2)}, u32[]{:S(2)}) collective-permute-start(f32[48,128]{1,0:T(8,128)S(1)} %get-tuple-element.23.refs_0_), channel_id=1, source_target_pairs={{0,8},{1,9},{2,10},{3,11},{4,12},{5,13},{6,14},{7,15},{8,0},{9,1},... | collective-permute-start | bytes 73736 | tf_op jit(solution)/shard_map/ppermute | solution.py:400
  69.6 3.5 %collective-permute-start.15 = (f32[48,128]{1,0:T(8,128)S(1)}, f32[48,128]{1,0:T(8,128)S(1)}, u32[]{:S(2)}, u32[]{:S(2)}) collective-permute-start(f32[48,128]{1,0:T(8,128)S(1)} %get-tuple-element.23.refs_0_), channel_id=1, source_target_pairs={{0,9},{1,8},{2,11},{3,10},{4,13},{5,12},{6,15},{7,14},{8,1},{9,0},... | collective-permute-start | bytes 73736 | tf_op jit(solution)/shard_map/ppermute | solution.py:400

commit v2 on v1

--- a/solution.py
+++ b/solution.py
@@ -112,14 +112,18 @@
         at = self.couple
         self.rhs_at = at if at % LANES + own <= LANES else round_up(at, LANES)
         self.couple_wide = round_up(self.rhs_at + own, LANES)
-        self.flips = [0, 2, 4, 6]
+        self.rest_couple = self.couple_wide - self.order[1]
+        self.rest_wide = self.rest_couple + sum(self.order[2:-1])
+        self.join_diag = self.order[1] + LANES
+        self.join_wide = self.join_diag + self.order[1]
+        self.couple_flips, self.diag_flips, self.flips = [0, 2, 1, 3], [0, 4, 1, 5], [0, 2, 4, 6]
 
     def shared(self, level):
         return [flip for flip in self.flips if flip < self.members[level]]
 
-    def open_bits(self, level):
+    def open_bits(self, level, shared):
         bits = range(self.members[level].bit_length() - 1)
-        return [bit for bit in bits if (1 << bit) not in (2, 4)]
+        return [bit for bit in bits if (1 << bit) not in shared]
 
     def local(self, level):
         position = lax.axis_index("leaf") * (self.total // self.leafs) + lax.axis_index("sub")
@@ -132,27 +136,41 @@
     return scratch[...].T
 
 
-def start_kernel(plan, rhs, coupling, wire, joined, scratch):
+def start_kernel(plan, rhs, wire, late, scratch):
     first = jnp.concatenate([rhs[0, 0], rhs[1, 0]], axis=0)
     first = transposed(first, scratch)
     padded = plan.groups * plan.group_rows
     blocks = [first[at : at + plan.group_rows] for at in range(0, padded, plan.group_rows)]
     packed = side_by_side(blocks, plan.width)
     wire[...] = jnp.broadcast_to(packed[None], wire.shape)
+    for part in range(2):
+        later = jnp.concatenate([rhs[part, level] for level in range(1, LEVELS)], axis=0)
+        late[part] = transposed(later, scratch)[0 : plan.rows]
+
+
+def cut_kernel(plan, coupling, diag, late, couple, diag_first, rest):
+    first = plan.order[1]
     whole = plan.couple // LANES * LANES
     tail = plan.couple - whole
     shift = plan.rhs_at % LANES
     for part in range(2):
-        later = jnp.concatenate([rhs[part, level] for level in range(1, LEVELS)], axis=0)
-        later = transposed(later, scratch)[0 : plan.rows]
-        joined[part, :, 0:whole] = coupling[part, :, 0:whole]
-        joined[part, :, plan.couple_wide - LANES :] = roll_right(later, shift)
+        couple[part, :, 0:first] = coupling[part, :, 0:first]
+        couple[part, :, first:] = late[part]
+        diag_first[part] = diag[part, :, plan.order[0] : plan.order[0] + first]
+        rest[part, :, 0 : whole - first] = coupling[part, :, first:whole]
+        start = plan.rhs_at // LANES * LANES - first
+        rest[part, :, start : start + LANES] = roll_right(late[part], shift)
         if tail:
-            joined[part, :, whole : whole + tail] = coupling[part, :, whole : whole + tail]
-
-
-def cut_kernel(plan, diag, middle):
-    middle[...] = diag[:, :, plan.order[0] : sum(plan.order[:-1])]
+            rest[part, :, whole - first : plan.couple - first] = coupling[part, :, whole:]
+        rest[part, :, plan.rest_couple :] = diag[
+            part, :, plan.order[0] + first : sum(plan.order[:-1])
+        ]
+
+
+def join_kernel(plan, couple, from_x, diag, from_y, joined):
+    for at, (left, right) in enumerate(((couple, diag), (from_x, from_y))):
+        joined[at, :, :, 0 : plan.join_diag] = left[...]
+        joined[at, :, :, plan.join_diag :] = right[...]
 
 
 def relay_kernel(plan, from_x, from_y, real, imag):
@@ -160,9 +178,15 @@
     imag[...] = from_y[1]
 
 
-def rhs_rows(plan, real, imag, level, shift_cols):
-    start = plan.rhs_at // LANES * LANES - shift_cols
-    offset = plan.rhs_at % LANES + plan.sources * (level - 1)
+def rest_join_kernel(plan, own, from_x, from_y, real, imag, held):
+    held[0] = own[...]
+    held[1] = from_x[...]
+    held[2] = from_y[...]
+    held[3, 0] = real[...]
+    held[3, 1] = imag[...]
+
+
+def rhs_rows(plan, real, imag, start, offset):
     re_part = roll_left(real[:, start : start + LANES], offset)
     im_part = roll_left(imag[:, start : start + LANES], offset - plan.sources)
     return jnp.where(lane_of(re_part.shape) < plan.sources, re_part, im_part)
@@ -196,53 +220,45 @@
     pack_all(plan, product(diag[0, :, 0:top], diag[1, :, 0:top], packed, plan.width), wire)
 
 
-def reduce_rows(plan, level, blocks, packed_first_col, packed):
+def reduce_rows(plan, level, blocks, packed):
+    first, start, offset = 0, plan.order[1], 0
+    if level > 1:
+        first = plan.couple_at[level] - plan.order[1]
+        start = plan.rhs_at // LANES * LANES - plan.order[1]
+        offset = plan.rhs_at % LANES + plan.sources * (level - 1)
     out = []
-    first = plan.couple_at[level] - packed_first_col
-    for real, imag in blocks:
+    for pair in blocks:
+        real, imag = pair.at[0], pair.at[1]
         cols = slice(first, first + plan.order[level])
         value = product(real[:, cols], imag[:, cols], packed, plan.width)
-        out.append(rhs_rows(plan, real, imag, level, packed_first_col) - value)
+        out.append(rhs_rows(plan, real, imag, start, offset) - value)
     return out
 
 
-def first_reduce_kernel(
-    plan, near, far, index, own, from_x, from_y, diag_re, diag_im, wire, top, rest, bounds
-):
+def pairs_of(near, far):
+    return [near.at[0], near.at[1], far.at[0], far.at[1]]
+
+
+def first_reduce_kernel(plan, near, far, index, joined, joined_far, wire, top, bounds):
     unpack_all(plan, near, far, top)
     gather_rows(
         top.reshape(plan.order[0], LANES), index, plan.couple_at[1], plan.order[1], bounds
     )
-    blocks = [
-        (own.at[0], own.at[1]),
-        (from_x.at[0], from_x.at[1]),
-        (from_y.at[0], from_y.at[1]),
-        (diag_re, diag_im),
-    ]
     packed = weights(bounds[...], plan.width)
-    wire[...] = side_by_side(reduce_rows(plan, 1, blocks, 0, packed), plan.width)
-    for at, (real, imag) in enumerate(blocks):
-        rest[at, 0] = real[:, plan.order[1] :]
-        rest[at, 1] = imag[:, plan.order[1] :]
+    blocks = pairs_of(joined, joined_far)
+    wire[...] = side_by_side(reduce_rows(plan, 1, blocks, packed), plan.width)
 
 
 def first_solve_kernel(plan, flips, *refs):
     wires, refs = refs[: len(flips)], refs[len(flips) :]
-    own, from_x, from_y, diag_re, diag_im, wire, rest, vector = refs
-    order = plan.order[1]
-    spread(wires, vector, 0, plan.local(1), flips, plan.shared(1), plan.rows, plan.width)
+    joined, joined_far, wire, vector = refs
+    cols = slice(plan.join_diag, plan.join_wide)
+    spread(wires, vector, 0, plan.local(1), flips, plan.couple_flips, plan.rows, plan.width)
     packed = weights(vector[...], plan.width)
-    blocks = [
-        (own.at[0], own.at[1]),
-        (from_x.at[0], from_x.at[1]),
-        (from_y.at[0], from_y.at[1]),
-        (diag_re, diag_im),
-    ]
-    solved = [product(re[:, 0:order], im[:, 0:order], packed, plan.width) for re, im in blocks]
+    solved = []
+    for pair in pairs_of(joined, joined_far):
+        solved.append(product(pair[0, :, cols], pair[1, :, cols], packed, plan.width))
     wire[...] = side_by_side(solved, plan.width)
-    for at, (real, imag) in enumerate(blocks):
-        rest[at, 0] = real[:, order:]
-        rest[at, 1] = imag[:, order:]
 
 
 def pack_owners(plan, row_map, local_rows, packing, out):
@@ -279,18 +295,17 @@
 
 def tail_kernel(plan, flips, *refs):
     wires, refs = refs[: len(flips)], refs[len(flips) :]
-    top, index, row_map, couple, couple_far, diag, diag_far, diag_own = refs[:8]
-    out, vector, bounds, front, local_rows, packing = refs[8:]
+    top, index, row_map, near, far, diag_own = refs[:6]
+    out, vector, bounds, front, local_rows, packing = refs[6:]
     rows, width = plan.rows, plan.width
     vector[0 : plan.order[0], :] = top[...]
-    spread(wires, vector, plan.order[0], plan.local(1), flips, plan.shared(1), rows, width)
-    cut = plan.order[1]
+    spread(wires, vector, plan.order[0], plan.local(1), flips, plan.diag_flips, rows, width)
 
     def held(level):
         found = []
         for at, flip in enumerate(plan.shared(level)):
-            found.append((flip, couple.at[at], diag.at[at]))
-            found.append((flip ^ 1, couple_far.at[at], diag_far.at[at]))
+            found.append((flip, near.at[at]))
+            found.append((flip ^ 1, far.at[at]))
         return found
 
     for level in range(2, LEVELS):
@@ -298,15 +313,16 @@
         local = plan.local(level)
         gather_rows(vector, index, plan.couple_at[level], order, bounds)
         packed = weights(bounds[0:order, :], width)
-        blocks = [(pair.at[0], pair.at[1]) for _, pair, _ in held(level)]
-        reduced = reduce_rows(plan, level, blocks, cut, packed)
-        for (flip, _, _), value in zip(held(level), reduced):
+        reduced = reduce_rows(plan, level, [pair for _, pair in held(level)], packed)
+        for (flip, _), value in zip(held(level), reduced):
             front[pl.ds(pl.multiple_of((local ^ flip) * rows, 8), rows), :] = value
         packed = weights(front[0:order, :], width)
         base = plan.ancestors[level]
         if level + 1 < LEVELS:
-            for flip, _, pair in held(level):
-                solved = product(pair[0], pair[1], packed, width)
+            start = plan.rest_couple + sum(plan.order[2:level])
+            for flip, pair in held(level):
+                cols = slice(start, start + order)
+                solved = product(pair[0, :, cols], pair[1, :, cols], packed, width)
                 place = pl.multiple_of(base + (local ^ flip) * rows, 8)
                 vector[pl.ds(place, rows), :] = solved
         else:
@@ -316,31 +332,30 @@
     pack_owners(plan, row_map, local_rows, packing, out)
 
 
-def reduce_kernel(plan, level, flips, *refs):
+def reduce_kernel(plan, level, flips, lane_flips, *refs):
     wires, refs = refs[: len(flips)], refs[len(flips) :]
-    top, index, couple, wire, vector, bounds = refs
-    rows, width = plan.rows, plan.width
-    vector[0 : plan.ancestors[level - 1], :] = top[...]
+    top, index, held, wire, vector, bounds = refs
+    upper = plan.ancestors[level - 1]
+    vector[0:upper, :] = top[...]
     spread(
-        wires, vector, plan.ancestors[level - 1], plan.local(level - 1), flips,
-        plan.shared(level - 1), rows, width,
+        wires, vector, upper, plan.local(level - 1), flips, lane_flips, plan.rows, plan.width
     )
     gather_rows(vector, index, plan.couple_at[level], plan.order[level], bounds)
-    blocks = [(couple.at[at, 0], couple.at[at, 1]) for at in range(len(plan.shared(level)))]
-    packed = weights(bounds[...], width)
-    wire[...] = side_by_side(reduce_rows(plan, level, blocks, plan.order[1], packed), width)
-
-
-def solve_kernel(plan, level, flips, first_col, *refs):
+    blocks = [held.at[at] for at in range(len(plan.shared(level)))]
+    packed = weights(bounds[...], plan.width)
+    wire[...] = side_by_side(reduce_rows(plan, level, blocks, packed), plan.width)
+
+
+def solve_kernel(plan, level, flips, *refs):
     wires, refs = refs[: len(flips)], refs[len(flips) :]
-    diag, wire, vector = refs
+    held, wire, vector = refs
     spread(wires, vector, 0, plan.local(level), flips, plan.shared(level), plan.rows, plan.width)
     packed = weights(vector[...], plan.width)
-    cols = slice(first_col, first_col + plan.order[level])
-    solved = [
-        product(diag[at, 0, :, cols], diag[at, 1, :, cols], packed, plan.width)
-        for at in range(len(plan.shared(level)))
-    ]
+    start = plan.rest_couple + sum(plan.order[2:level])
+    cols = slice(start, start + plan.order[level])
+    solved = []
+    for at in range(len(plan.shared(level))):
+        solved.append(product(held[at, 0, :, cols], held[at, 1, :, cols], packed, plan.width))
     wire[...] = side_by_side(solved, plan.width)
 
 
@@ -399,8 +414,8 @@
         route = [(device, device ^ flip) for device in range(total)]
         return lax.ppermute(array, AXES, route)
 
-    def exchange(wire, level):
-        bits = plan.open_bits(level)
+    def exchange(wire, level, shared):
+        bits = plan.open_bits(level, shared)
         flips = [0]
         for bit in bits:
             flips = flips + [flip ^ (1 << bit) for flip in flips]
@@ -415,70 +430,69 @@
         near = lax.all_to_all(wire, "leaf", 0, 0)
         return near, flip_to(near, 1)
 
-    def neighbours(array):
-        return array, flip_to(array, 2), flip_to(array, 4)
-
-    def beyond(pieces):
-        own, from_x, from_y = pieces
-        real, imag = call(relay_kernel, plan, [own.shape[1:]] * 2, [], [from_x, from_y])
-        real, imag = flip_to(real, 4), flip_to(imag, 2)
-        return own, from_x, from_y, real, imag
-
-    wire, joined = call(
-        start_kernel, plan, [wire_shape, (2, rows, plan.couple_wide)], [(LANES, LANES)],
-        [right_sides, coupling],
-    )
-    (diag_mid,) = call(cut_kernel, plan, [(2, rows, sum(order[1:-1]))], [], [diag_inverse])
+    part = (2, rows)
+    wire, late = call(
+        start_kernel, plan, [wire_shape, (*part, LANES)], [(LANES, LANES)], [right_sides]
+    )
+    couple, diag_first, rest = call(
+        cut_kernel, plan,
+        [(*part, plan.join_diag), (*part, order[1]), (*part, plan.rest_wide)], [],
+        [coupling, diag_inverse, late],
+    )
     gathered = to_all(wire)
-    couple = beyond(neighbours(joined))
+    from_x, from_y = flip_to(couple, 2), flip_to(diag_first, 4)
     (wire,) = call(top_kernel, plan, [wire_shape], [whole_shape], [*gathered, diag_inverse])
     gathered = to_all(wire)
-    diag = beyond(neighbours(diag_mid))
-    wire, top, couple_rest = call(
-        first_reduce_kernel, plan,
-        [block, whole_shape, (4, 2, rows, plan.couple_wide - order[1])],
-        [(order[1], LANES)],
-        [*gathered, boundary, *couple], scalars=(2,),
+    (joined,) = call(
+        join_kernel, plan, [(2, *part, plan.join_wide)], [],
+        [couple, from_x, diag_first, from_y],
+    )
+    joined_far = flip_to(joined, 1)
+    rest_x, rest_y = flip_to(rest, 2), flip_to(rest, 4)
+    wire, top = call(
+        first_reduce_kernel, plan, [block, whole_shape], [(order[1], LANES)],
+        [*gathered, boundary, joined, joined_far], scalars=(2,),
     )
     top = top.reshape(order[0], LANES)
-    wires, flips = exchange(wire, 1)
-    wire, diag_rest = call(
-        first_solve_kernel, plan, [block, (4, 2, rows, diag_mid.shape[2] - order[1])],
-        [(order[1], LANES)], [*wires, *diag], static=(flips,),
-    )
-    wires, flips = exchange(wire, 1)
+    wires, flips = exchange(wire, 1, (1, 2))
+    real, imag = call(relay_kernel, plan, [(rows, plan.rest_wide)] * 2, [], [rest_x, rest_y])
+    real, imag = flip_to(real, 4), flip_to(imag, 2)
+    (wire,) = call(
+        first_solve_kernel, plan, [block], [(order[1], LANES)],
+        [*wires, joined, joined_far], static=(flips,),
+    )
+    wires, flips = exchange(wire, 1, (1, 4))
+    (held,) = call(
+        rest_join_kernel, plan, [(4, *part, plan.rest_wide)], [],
+        [rest, rest_x, rest_y, real, imag],
+    )
     if plan.members[2] <= 8:
-        couple_far = flip_to(couple_rest, 1)
-        diag_far = flip_to(diag_rest, 1)
+        held_far = flip_to(held, 1)
         (packed,) = call(
             tail_kernel, plan, [(leafs, owner_rows, LANES)],
             [
                 (plan.ancestors[LEVELS - 1], LANES), (order[2], LANES), (order[2], LANES),
                 (LEVELS * rows, LANES), packing,
             ],
-            [
-                *wires, top, boundary, plane_map, couple_rest, couple_far, diag_rest, diag_far,
-                diag_inverse,
-            ],
+            [*wires, top, boundary, plane_map, held, held_far, diag_inverse],
             scalars=(len(flips) + 1, len(flips) + 2), static=(flips,),
         )
     else:
-        first_col = 0
+        lane_flips = plan.diag_flips
         for level in range(2, LEVELS):
             wire, top = call(
                 reduce_kernel, plan, [block, (plan.ancestors[level], LANES)],
-                [(order[level], LANES)],
-                [*wires, top, boundary, couple_rest], scalars=(len(flips) + 1,),
-                static=(level, flips),
+                [(order[level], LANES)], [*wires, top, boundary, held],
+                scalars=(len(flips) + 1,), static=(level, flips, lane_flips),
             )
-            wires, flips = exchange(wire, level)
+            lane_flips = plan.shared(level)
+            wires, flips = exchange(wire, level, (2, 4))
             if level + 1 < LEVELS:
                 (wire,) = call(
                     solve_kernel, plan, [block], [(order[level], LANES)],
-                    [*wires, diag_rest], static=(level, flips, first_col),
+                    [*wires, held], static=(level, flips),
                 )
-                first_col += order[level]
-                wires, flips = exchange(wire, level)
+                wires, flips = exchange(wire, level, (2, 4))
         (packed,) = call(
             last_kernel, plan, [(leafs, owner_rows, LANES)],
             [(order[-1], LANES), (LEVELS * rows, LANES), packing],

time: 90.9 us -> 92.5 us (1.018)
  blocking collectives: 25.6 us -> 34.5 us
  starting transfers between devices: 20.8 us -> 15.9 us
  Pallas kernels: 13.8 us -> 11.1 us
    all_to_all x1 -> x2, blocking collectives: 13.8 us -> 23.6 us  [to_all(): near = lax.all_to_all(wire, 'leaf', 0, 0)]
    all_to_all x1 -> x0, starting transfers between devices: 5.99 us -> none  [to_all(): near = lax.all_to_all(wire, 'leaf', 0, 0)]
    ppermute x18 -> x16, waiting for transfers between devices: 24.2 us -> 27.4 us  [flip_to(): return lax.ppermute(array, AXES, route)]
    all_to_all x1 -> x0, waiting for transfers between devices: 2.81 us -> none  [to_all(): near = lax.all_to_all(wire, 'leaf', 0, 0)]
    pallas_call x9 -> x10, Pallas kernels: 13.8 us -> 11.1 us  [call(): pl.pallas_call(functools.partial(kernel, plan, *static), out_shape=shapes...]
    ppermute x18 -> x16, starting transfers between devices: 14.8 us -> 15.9 us  [flip_to(): return lax.ppermute(array, AXES, route)]
    all_to_all x1, blocking collectives: 11.8 us -> 10.9 us  [local(): received = lax.all_to_all(packed, 'leaf', 0, 0)]
  transfers between devices with their start and end apart: 19 -> 16, of which waited for: 10 -> 14; matrix products, arithmetic and copies ran while one was open for 0% -> 0% of each run, Pallas kernels for 8% -> 6%
where the time goes in v2:
time: 92.5 us; the launch traced here: 92.2 us
  blocking collectives  34.5 us (37%)
  waiting for transfers between devices  27.4 us (30%)
  starting transfers between devices  15.9 us (17%)
  Pallas kernels  11.1 us (12%)
  local copies, waits for them, and re-layouts  3.16 us (3%)
    ppermute x16, waiting for transfers between devices, flip_to(): return lax.ppermute(array, AXES, route)  27.4 us
    all_to_all x2, blocking collectives, to_all(): near = lax.all_to_all(wire, 'leaf', 0, 0)  23.6 us
    ppermute x16, starting transfers between devices, flip_to(): return lax.ppermute(array, AXES, route)  15.9 us
    pallas_call x10, Pallas kernels, call(): pl.pallas_call(functools.partial(kernel, plan, *static), out_shape=shapes...  11.1 us
    all_to_all x1, blocking collectives, local(): received = lax.all_to_all(packed, 'leaf', 0, 0)  10.9 us
    unnamed x12, local copies, waits for them, and re-layouts  3.16 us
  transfers between devices with their start and end apart: 16, of which 14 were waited for; matrix products, arithmetic and copies ran while one was open for 0% of the time, Pallas kernels for 6%

profile of v2, /device:TPU:0, one launch (start us, length us, event | category | flops | bytes accessed | tf_op | source)
XLA Modules:
  0.0 92.2 jit_solution(12759540912244608201)
XLA Ops:
  0.0 0.0 copy-start.3
  0.0 0.8 copy-done.3
  0.8 0.2 shard_map.55
  1.0 0.0 copy-start
  1.0 1.3 %copy-done = f32[2,48,2880]{2,1,0:T(8,128)S(1)} copy-done((f32[2,48,2880]{2,1,0:T(8,128)S(1)}, f32[2,48,2880]{2,1,0:T(8,128)}, u32[]{:S(2)}) %copy-start) | copy-done | bytes 1105944
  2.3 0.0 copy-start.2
  2.3 1.0 %copy-done.2 = f32[2,48,1344]{2,1,0:T(8,128)S(1)} copy-done((f32[2,48,1344]{2,1,0:T(8,128)S(1)}, f32[2,48,1344]{2,1,0:T(8,128)}, u32[]{:S(2)}) %copy-start.2) | copy-done | bytes 516120
  3.3 0.1 shard_map.57
  3.4 3.0 %collective-permute-start.11 = (f32[2,48,1024]{2,1,0:T(8,128)S(1)}, f32[2,48,1024]{2,1,0:T(8,128)S(1)}, u32[]{:S(2)}, u32[]{:S(2)}) collective-permute-start(f32[2,48,1024]{2,1,0:T(8,128)S(1)} %get-tuple-element.20.own), channel_id=1, source_target_pairs={{0,2},{1,3},{2,0},{3,1},{4,6},{5,7},{6,4},{7,5},{8,10},{9,11},{10,... | collective-permute-start | bytes 1179656 | tf_op jit(solution)/shard_map/ppermute | solution.py:415
  6.5 1.5 %collective-permute-start.12 = (f32[2,48,1024]{2,1,0:T(8,128)S(1)}, f32[2,48,1024]{2,1,0:T(8,128)S(1)}, u32[]{:S(2)}, u32[]{:S(2)}) collective-permute-start(f32[2,48,1024]{2,1,0:T(8,128)S(1)} %get-tuple-element.20.own), channel_id=1, source_target_pairs={{0,4},{1,5},{2,6},{3,7},{4,0},{5,1},{6,2},{7,3},{8,12},{9,13},{10,... | collective-permute-start | bytes 1179656 | tf_op jit(solution)/shard_map/ppermute | solution.py:415
  8.0 7.6 %collective-permute-done.11.from_x = f32[2,48,1024]{2,1,0:T(8,128)S(1)} collective-permute-done((f32[2,48,1024]{2,1,0:T(8,128)S(1)}, f32[2,48,1024]{2,1,0:T(8,128)S(1)}, u32[]{:S(2)}, u32[]{:S(2)}) %collective-permute-start.11) | collective-permute-done | bytes 393248 | tf_op jit(solution)/shard_map/ppermute | solution.py:415
  15.6 1.5 %collective-permute-done.12.from_y = f32[2,48,1024]{2,1,0:T(8,128)S(1)} collective-permute-done((f32[2,48,1024]{2,1,0:T(8,128)S(1)}, f32[2,48,1024]{2,1,0:T(8,128)S(1)}, u32[]{:S(2)}, u32[]{:S(2)}) %collective-permute-start.12) | collective-permute-done | bytes 393248 | tf_op jit(solution)/shard_map/ppermute | solution.py:415
  17.1 1.6 %collective-permute-start.13 = (f32[48,1024]{1,0:T(8,128)S(1)}, f32[48,1024]{1,0:T(8,128)S(1)}, u32[]{:S(2)}, u32[]{:S(2)}) collective-permute-start(f32[48,1024]{1,0:T(8,128)S(1)} %get-tuple-element.21), channel_id=1, source_target_pairs={{0,4},{1,5},{2,6},{3,7},{4,0},{5,1},{6,2},{7,3},{8,12},{9,13},{10,... | collective-permute-start | bytes 589832 | tf_op jit(solution)/shard_map/ppermute | solution.py:415
  18.7 0.5 collective-permute-start.14
  19.2 1.5 %collective-permute-start.2 = (f32[2,48,896]{2,1,0:T(8,128)S(1)}, f32[2,48,896]{2,1,0:T(8,128)S(1)}, u32[]{:S(2)}, u32[]{:S(2)}) collective-permute-start(f32[2,48,896]{2,1,0:T(8,128)S(1)} %get-tuple-element.16.couple), channel_id=1, source_target_pairs={{0,2},{1,3},{2,0},{3,1},{4,6},{5,7},{6,4},{7,5},{8,10},{9,11},{10,... | collective-permute-start | bytes 1032200 | tf_op jit(solution)/shard_map/ppermute | solution.py:415
  20.7 0.5 collective-permute-start.3
  21.2 3.3 %collective-permute-done.13.real = f32[48,1024]{1,0:T(8,128)S(1)} collective-permute-done((f32[48,1024]{1,0:T(8,128)S(1)}, f32[48,1024]{1,0:T(8,128)S(1)}, u32[]{:S(2)}, u32[]{:S(2)}) %collective-permute-start.13) | collective-permute-done | bytes 196640 | tf_op jit(solution)/shard_map/ppermute | solution.py:415
  24.5 2.0 %collective-permute-done.14.imag = f32[48,1024]{1,0:T(8,128)S(1)} collective-permute-done((f32[48,1024]{1,0:T(8,128)S(1)}, f32[48,1024]{1,0:T(8,128)S(1)}, u32[]{:S(2)}, u32[]{:S(2)}) %collective-permute-start.14) | collective-permute-done | bytes 196640 | tf_op jit(solution)/shard_map/ppermute | solution.py:415
  26.4 0.1 shard_map.62.refs_7_
  26.5 0.0 copy-start.1
  26.5 0.1 collective-permute-start.15
  26.6 2.5 %collective-permute-done.3.from_y = f32[2,48,768]{2,1,0:T(8,128)S(1)} collective-permute-done((f32[2,48,768]{2,1,0:T(8,128)S(1)}, f32[2,48,768]{2,1,0:T(8,128)S(1)}, u32[]{:S(2)}, u32[]{:S(2)}) %collective-permute-start.3) | collective-permute-done | bytes 294944 | tf_op jit(solution)/shard_map/ppermute | solution.py:415
  29.1 2.1 %collective-permute-done.2.from_x = f32[2,48,896]{2,1,0:T(8,128)S(1)} collective-permute-done((f32[2,48,896]{2,1,0:T(8,128)S(1)}, f32[2,48,896]{2,1,0:T(8,128)S(1)}, u32[]{:S(2)}, u32[]{:S(2)}) %collective-permute-start.2) | collective-permute-done | bytes 344096 | tf_op jit(solution)/shard_map/ppermute | solution.py:415
  31.3 0.1 shard_map.58.joined.refs_4_
  31.3 0.0 copy-start.4
  31.4 0.1 collective-permute-start.4
  31.4 12.9 %all_to_all.15.near = f32[16,16,128]{2,1,0:T(8,128)S(1)} all-to-all(f32[16,16,128]{2,1,0:T(8,128)S(1)} %get-tuple-element.14), channel_id=1, replica_groups=mesh['leaf'=16,'sub'=2] {'leaf'}, dimensions={0} | all-to-all | bytes 262144 | tf_op jit(solution)/shard_map/all_to_all | solution.py:430
  44.3 0.0 collective-permute-start
  44.3 1.3 %collective-permute-done.far = f32[16,16,128]{2,1,0:T(8,128)S(1)} collective-permute-done((f32[16,16,128]{2,1,0:T(8,128)S(1)}, f32[16,16,128]{2,1,0:T(8,128)S(1)}, u32[]{:S(2)}, u32[]{:S(2)}) %collective-permute-start) | collective-permute-done | bytes 131104 | tf_op jit(solution)/shard_map/ppermute | solution.py:415
  45.6 0.0 copy-done.1
  45.7 1.1 %shard_map.56 = f32[16,16,128]{2,1,0:T(8,128)S(1)} custom-call(f32[16,16,128]{2,1,0:T(8,128)S(1)} %all_to_all.15.near, f32[16,16,128]{2,1,0:T(8,128)S(1)} %collective-permute-done.far, f32[2,48,2880]{2,1,0:T(8,128)S(1)} %copy-done.1), custom_call_target="tpu_custom_call" | custom-call | tf_op jit(solution)/shard_map/pallas_call | solution.py:390
  46.7 10.8 %all_to_all.16.near = f32[16,16,128]{2,1,0:T(8,128)S(1)} all-to-all(f32[16,16,128]{2,1,0:T(8,128)S(1)} %shard_map.56), channel_id=1, replica_groups=mesh['leaf'=16,'sub'=2] {'leaf'}, dimensions={0} | all-to-all | bytes 262144 | tf_op jit(solution)/shard_map/all_to_all | solution.py:430
  57.5 0.0 collective-permute-start.1
  57.5 1.3 %collective-permute-done.1.far = f32[16,16,128]{2,1,0:T(8,128)S(1)} collective-permute-done((f32[16,16,128]{2,1,0:T(8,128)S(1)}, f32[16,16,128]{2,1,0:T(8,128)S(1)}, u32[]{:S(2)}, u32[]{:S(2)}) %collective-permute-start.1) | collective-permute-done | bytes 131104 | tf_op jit(solution)/shard_map/ppermute | solution.py:415
  58.8 0.0 collective-permute-done.4.joined_far.refs_5_
  58.9 0.0 copy-done.4
  58.9 2.8 %shard_map.59 = (f32[48,128]{1,0:T(8,128)S(1)}, f32[16,2,48,128]{3,2,1,0:T(8,128)S(1)}) custom-call(f32[16,16,128]{2,1,0:T(8,128)S(1)} %all_to_all.16.near, f32[16,16,128]{2,1,0:T(8,128)S(1)} %collective-permute-done.1.far, s32[1,1344]{1,0:T(1,128)S(1)} %copy-done.4, f32[2,2,48,1664]{3,2,1,0:T(8,128)S(1)} %shard_map.58.joined.refs_4_, ...), custom_call_target="tpu_custom_call" | custom-call | tf_op jit(solution)/shard_map/pallas_call | solution.py:390
  61.7 0.0 copy-start.5
  61.7 0.8 collective-permute-start.5
  62.5 0.9 collective-permute-start.6
  63.4 1.9 %collective-permute-start.7 = (f32[48,128]{1,0:T(8,128)S(1)}, f32[48,128]{1,0:T(8,128)S(1)}, u32[]{:S(2)}, u32[]{:S(2)}) collective-permute-start(f32[48,128]{1,0:T(8,128)S(1)} %get-tuple-element.18.refs_0_), channel_id=1, source_target_pairs={{0,12},{1,13},{2,14},{3,15},{4,8},{5,9},{6,10},{7,11},{8,4},{9,5},... | collective-permute-start | bytes 73736 | tf_op jit(solution)/shard_map/ppermute | solution.py:415
  65.3 0.3 collective-permute-done.5.refs_1_
  65.6 0.8 collective-permute-done.6.refs_2_
  66.4 1.7 %collective-permute-done.7.refs_3_ = f32[48,128]{1,0:T(8,128)S(1)} collective-permute-done((f32[48,128]{1,0:T(8,128)S(1)}, f32[48,128]{1,0:T(8,128)S(1)}, u32[]{:S(2)}, u32[]{:S(2)}) %collective-permute-start.7) | collective-permute-done | bytes 24608 | tf_op jit(solution)/shard_map/ppermute | solution.py:415
  68.1 1.1 %shard_map.60.refs_0_ = f32[48,128]{1,0:T(8,128)S(1)} custom-call(f32[48,128]{1,0:T(8,128)S(1)} %get-tuple-element.18.refs_0_, f32[48,128]{1,0:T(8,128)S(1)} %collective-permute-done.5.refs_1_, f32[48,128]{1,0:T(8,128)S(1)} %collective-permute-done.6.refs_2_, f32[48,128]{1,0:T(8,128)S(1)} %collective-permute-done.7.refs_3_, ...), custom_call_target="tpu_custom_call" | custom-call | tf_op jit(solution)/shard_map/pallas_call | solution.py:390
  69.2 1.2 %collective-permute-start.10 = (f32[48,128]{1,0:T(8,128)S(1)}, f32[48,128]{1,0:T(8,128)S(1)}, u32[]{:S(2)}, u32[]{:S(2)}) collective-permute-start(f32[48,128]{1,0:T(8,128)S(1)} %shard_map.60.refs_0_), channel_id=1, source_target_pairs={{0,10},{1,11},{2,8},{3,9},{4,14},{5,15},{6,12},{7,13},{8,2},{9,3},... | collective-permute-start | bytes 73736 | tf_op jit(solution)/shard_map/ppermute | solution.py:415
  70.4 1.5 %collective-permute-start.8 = (f32[48,128]{1,0:T(8,128)S(1)}, f32[48,128]{1,0:T(8,128)S(1)}, u32[]{:S(2)}, u32[]{:S(2)}) collective-permute-start(f32[48,128]{1,0:T(8,128)S(1)} %shard_map.60.refs_0_), channel_id=1, source_target_pairs={{0,2},{1,3},{2,0},{3,1},{4,6},{5,7},{6,4},{7,5},{8,10},{9,11},{10,... | collective-permute-start | bytes 73736 | tf_op jit(solution)/shard_map/ppermute | solution.py:415
  71.9 0.9 collective-permute-start.9
  72.7 1.2 %collective-permute-done.10.refs_3_ = f32[48,128]{1,0:T(8,128)S(1)} collective-permute-done((f32[48,128]{1,0:T(8,128)S(1)}, f32[48,128]{1,0:T(8,128)S(1)}, u32[]{:S(2)}, u32[]{:S(2)}) %collective-permute-start.10) | collective-permute-done | bytes 24608 | tf_op jit(solution)/shard_map/ppermute | solution.py:415
  74.0 0.3 collective-permute-done.8.refs_1_
  74.2 1.5 %collective-permute-done.9.refs_2_ = f32[48,128]{1,0:T(8,128)S(1)} collective-permute-done((f32[48,128]{1,0:T(8,128)S(1)}, f32[48,128]{1,0:T(8,128)S(1)}, u32[]{:S(2)}, u32[]{:S(2)}) %collective-permute-start.9) | collective-permute-done | bytes 24608 | tf_op jit(solution)/shard_map/ppermute | solution.py:415
  75.7 0.0 collective-permute-done.15.refs_8_
  75.7 0.0 copy-done.5
  75.7 4.8 %shard_map.63 = f32[16,3,128]{2,1,0:T(4,128)S(1)} custom-call(f32[48,128]{1,0:T(8,128)S(1)} %shard_map.60.refs_0_, f32[48,128]{1,0:T(8,128)S(1)} %collective-permute-done.8.refs_1_, f32[48,128]{1,0:T(8,128)S(1)} %collective-permute-done.9.refs_2_, f32[48,128]{1,0:T(8,128)S(1)} %collective-permute-done.10.refs_3_, f32[1536,128]{1,0:T(8,128)S(1)} %bitcast.2, ...), custom_call_target="tpu_custom_call" | custom-call | tf_op jit(solution)/shard_map/pallas_call | solution.py:390
  80.5 10.9 %all_to_all.17.received = f32[16,3,128]{2,1,0:T(4,128)S(1)} all-to-all(f32[16,3,128]{2,1,0:T(4,128)S(1)} %shard_map.63), channel_id=1, replica_groups=mesh['leaf'=16,'sub'=2] {'leaf'}, dimensions={0} | all-to-all | bytes 49152 | tf_op jit(solution)/shard_map/all_to_all | solution.py:501
  91.4 0.8 shard_map.64
  (1 shorter events, 0.0 us)
Async XLA Ops:
  0.0 0.8 copy-start.3
  1.0 1.3 %copy-start = (f32[2,48,2880]{2,1,0:T(8,128)S(1)}, f32[2,48,2880]{2,1,0:T(8,128)}, u32[]{:S(2)}) copy-start(f32[2,48,2880]{2,1,0:T(8,128)} %refs_9_.1) | copy-start | bytes 3317764
  2.3 1.0 %copy-start.2 = (f32[2,48,1344]{2,1,0:T(8,128)S(1)}, f32[2,48,1344]{2,1,0:T(8,128)}, u32[]{:S(2)}) copy-start(f32[2,48,1344]{2,1,0:T(8,128)} %coupling.1) | copy-start | bytes 1548292
  3.4 12.1 %collective-permute-start.11 = (f32[2,48,1024]{2,1,0:T(8,128)S(1)}, f32[2,48,1024]{2,1,0:T(8,128)S(1)}, u32[]{:S(2)}, u32[]{:S(2)}) collective-permute-start(f32[2,48,1024]{2,1,0:T(8,128)S(1)} %get-tuple-element.20.own), channel_id=1, source_target_pairs={{0,2},{1,3},{2,0},{3,1},{4,6},{5,7},{6,4},{7,5},{8,10},{9,11},{10,... | collective-permute-start | bytes 1179656 | tf_op jit(solution)/shard_map/ppermute | solution.py:415
  6.5 10.6 %collective-permute-start.12 = (f32[2,48,1024]{2,1,0:T(8,128)S(1)}, f32[2,48,1024]{2,1,0:T(8,128)S(1)}, u32[]{:S(2)}, u32[]{:S(2)}) collective-permute-start(f32[2,48,1024]{2,1,0:T(8,128)S(1)} %get-tuple-element.20.own), channel_id=1, source_target_pairs={{0,4},{1,5},{2,6},{3,7},{4,0},{5,1},{6,2},{7,3},{8,12},{9,13},{10,... | collective-permute-start | bytes 1179656 | tf_op jit(solution)/shard_map/ppermute | solution.py:415
  17.1 7.4 %collective-permute-start.13 = (f32[48,1024]{1,0:T(8,128)S(1)}, f32[48,1024]{1,0:T(8,128)S(1)}, u32[]{:S(2)}, u32[]{:S(2)}) collective-permute-start(f32[48,1024]{1,0:T(8,128)S(1)} %get-tuple-element.21), channel_id=1, source_target_pairs={{0,4},{1,5},{2,6},{3,7},{4,0},{5,1},{6,2},{7,3},{8,12},{9,13},{10,... | collective-permute-start | bytes 589832 | tf_op jit(solution)/shard_map/ppermute | solution.py:415
  18.7 7.8 %collective-permute-start.14 = (f32[48,1024]{1,0:T(8,128)S(1)}, f32[48,1024]{1,0:T(8,128)S(1)}, u32[]{:S(2)}, u32[]{:S(2)}) collective-permute-start(f32[48,1024]{1,0:T(8,128)S(1)} %get-tuple-element.22), channel_id=1, source_target_pairs={{0,2},{1,3},{2,0},{3,1},{4,6},{5,7},{6,4},{7,5},{8,10},{9,11},{10,... | collective-permute-start | bytes 589832 | tf_op jit(solution)/shard_map/ppermute | solution.py:415
  19.2 12.1 %collective-permute-start.2 = (f32[2,48,896]{2,1,0:T(8,128)S(1)}, f32[2,48,896]{2,1,0:T(8,128)S(1)}, u32[]{:S(2)}, u32[]{:S(2)}) collective-permute-start(f32[2,48,896]{2,1,0:T(8,128)S(1)} %get-tuple-element.16.couple), channel_id=1, source_target_pairs={{0,2},{1,3},{2,0},{3,1},{4,6},{5,7},{6,4},{7,5},{8,10},{9,11},{10,... | collective-permute-start | bytes 1032200 | tf_op jit(solution)/shard_map/ppermute | solution.py:415
  20.7 8.4 %collective-permute-start.3 = (f32[2,48,768]{2,1,0:T(8,128)S(1)}, f32[2,48,768]{2,1,0:T(8,128)S(1)}, u32[]{:S(2)}, u32[]{:S(2)}) collective-permute-start(f32[2,48,768]{2,1,0:T(8,128)S(1)} %get-tuple-element.17.diag), channel_id=1, source_target_pairs={{0,4},{1,5},{2,6},{3,7},{4,0},{5,1},{6,2},{7,3},{8,12},{9,13},{10,... | collective-permute-start | bytes 884744 | tf_op jit(solution)/shard_map/ppermute | solution.py:415
  26.5 19.1 %copy-start.1 = (f32[2,48,2880]{2,1,0:T(8,128)S(1)}, f32[2,48,2880]{2,1,0:T(8,128)}, u32[]{:S(2)}) copy-start(f32[2,48,2880]{2,1,0:T(8,128)} %refs_9_.1) | copy-start | bytes 3317764
  26.5 49.2 %collective-permute-start.15 = (f32[4,2,48,1024]{3,2,1,0:T(8,128)S(1)}, f32[4,2,48,1024]{3,2,1,0:T(8,128)S(1)}, u32[]{:S(2)}, u32[]{:S(2)}) collective-permute-start(f32[4,2,48,1024]{3,2,1,0:T(8,128)S(1)} %shard_map.62.refs_7_), channel_id=1, source_target_pairs={{0,1},{1,0},{2,3},{3,2},{4,5},{5,4},{6,7},{7,6},{8,9},{9,8},{10,11... | collective-permute-start | bytes 4718600 | tf_op jit(solution)/shard_map/ppermute | solution.py:415
  31.3 27.5 %copy-start.4 = (s32[1,1344]{1,0:T(1,128)S(1)}, s32[1,1344]{1,0:T(1,128)}, u32[]{:S(2)}) copy-start(s32[1,1344]{1,0:T(1,128)} %refs_5_.1) | copy-start | bytes 16132
  31.4 27.5 %collective-permute-start.4 = (f32[2,2,48,1664]{3,2,1,0:T(8,128)S(1)}, f32[2,2,48,1664]{3,2,1,0:T(8,128)S(1)}, u32[]{:S(2)}, u32[]{:S(2)}) collective-permute-start(f32[2,2,48,1664]{3,2,1,0:T(8,128)S(1)} %shard_map.58.joined.refs_4_), channel_id=1, source_target_pairs={{0,1},{1,0},{2,3},{3,2},{4,5},{5,4},{6,7},{7,6},{8,9},{9,8},{10,11... | collective-permute-start | bytes 3833864 | tf_op jit(solution)/shard_map/ppermute | solution.py:415
  44.3 1.3 %collective-permute-start = (f32[16,16,128]{2,1,0:T(8,128)S(1)}, f32[16,16,128]{2,1,0:T(8,128)S(1)}, u32[]{:S(2)}, u32[]{:S(2)}) collective-permute-start(f32[16,16,128]{2,1,0:T(8,128)S(1)} %all_to_all.15.near), channel_id=1, source_target_pairs={{0,1},{1,0},{2,3},{3,2},{4,5},{5,4},{6,7},{7,6},{8,9},{9,8},{10,11... | collective-permute-start | bytes 393224 | tf_op jit(solution)/shard_map/ppermute | solution.py:415
  57.5 1.3 %collective-permute-start.1 = (f32[16,16,128]{2,1,0:T(8,128)S(1)}, f32[16,16,128]{2,1,0:T(8,128)S(1)}, u32[]{:S(2)}, u32[]{:S(2)}) collective-permute-start(f32[16,16,128]{2,1,0:T(8,128)S(1)} %all_to_all.16.near), channel_id=1, source_target_pairs={{0,1},{1,0},{2,3},{3,2},{4,5},{5,4},{6,7},{7,6},{8,9},{9,8},{10,11... | collective-permute-start | bytes 393224 | tf_op jit(solution)/shard_map/ppermute | solution.py:415
  61.7 14.0 %copy-start.5 = (s32[1,192]{1,0:T(1,128)S(1)}, s32[1,192]{1,0:T(1,128)}, u32[]{:S(2)}) copy-start(s32[1,192]{1,0:T(1,128)} %refs_6_.1) | copy-start | bytes 2308
  61.7 3.9 %collective-permute-start.5 = (f32[48,128]{1,0:T(8,128)S(1)}, f32[48,128]{1,0:T(8,128)S(1)}, u32[]{:S(2)}, u32[]{:S(2)}) collective-permute-start(f32[48,128]{1,0:T(8,128)S(1)} %get-tuple-element.18.refs_0_), channel_id=1, source_target_pairs={{0,4},{1,5},{2,6},{3,7},{4,0},{5,1},{6,2},{7,3},{8,12},{9,13},{10,... | collective-permute-start | bytes 73736 | tf_op jit(solution)/shard_map/ppermute | solution.py:415
  62.5 3.9 %collective-permute-start.6 = (f32[48,128]{1,0:T(8,128)S(1)}, f32[48,128]{1,0:T(8,128)S(1)}, u32[]{:S(2)}, u32[]{:S(2)}) collective-permute-start(f32[48,128]{1,0:T(8,128)S(1)} %get-tuple-element.18.refs_0_), channel_id=1, source_target_pairs={{0,8},{1,9},{2,10},{3,11},{4,12},{5,13},{6,14},{7,15},{8,0},{9,1},... | collective-permute-start | bytes 73736 | tf_op jit(solution)/shard_map/ppermute | solution.py:415
  63.4 4.7 %collective-permute-start.7 = (f32[48,128]{1,0:T(8,128)S(1)}, f32[48,128]{1,0:T(8,128)S(1)}, u32[]{:S(2)}, u32[]{:S(2)}) collective-permute-start(f32[48,128]{1,0:T(8,128)S(1)} %get-tuple-element.18.refs_0_), channel_id=1, source_target_pairs={{0,12},{1,13},{2,14},{3,15},{4,8},{5,9},{6,10},{7,11},{8,4},{9,5},... | collective-permute-start | bytes 73736 | tf_op jit(solution)/shard_map/ppermute | solution.py:415
  69.2 4.8 %collective-permute-start.10 = (f32[48,128]{1,0:T(8,128)S(1)}, f32[48,128]{1,0:T(8,128)S(1)}, u32[]{:S(2)}, u32[]{:S(2)}) collective-permute-start(f32[48,128]{1,0:T(8,128)S(1)} %shard_map.60.refs_0_), channel_id=1, source_target_pairs={{0,10},{1,11},{2,8},{3,9},{4,14},{5,15},{6,12},{7,13},{8,2},{9,3},... | collective-permute-start | bytes 73736 | tf_op jit(solution)/shard_map/ppermute | solution.py:415
  70.4 3.8 %collective-permute-start.8 = (f32[48,128]{1,0:T(8,128)S(1)}, f32[48,128]{1,0:T(8,128)S(1)}, u32[]{:S(2)}, u32[]{:S(2)}) collective-permute-start(f32[48,128]{1,0:T(8,128)S(1)} %shard_map.60.refs_0_), channel_id=1, source_target_pairs={{0,2},{1,3},{2,0},{3,1},{4,6},{5,7},{6,4},{7,5},{8,10},{9,11},{10,... | collective-permute-start | bytes 73736 | tf_op jit(solution)/shard_map/ppermute | solution.py:415
  71.9 3.8 %collective-permute-start.9 = (f32[48,128]{1,0:T(8,128)S(1)}, f32[48,128]{1,0:T(8,128)S(1)}, u32[]{:S(2)}, u32[]{:S(2)}) collective-permute-start(f32[48,128]{1,0:T(8,128)S(1)} %shard_map.60.refs_0_), channel_id=1, source_target_pairs={{0,8},{1,9},{2,10},{3,11},{4,12},{5,13},{6,14},{7,15},{8,0},{9,1},... | collective-permute-start | bytes 73736 | tf_op jit(solution)/shard_map/ppermute | solution.py:415
